TPU v7x, 512 devices: a whole 4x4x16 slice. The times are simulated.
512 devices in a mesh: module: 8 (over x, y_lo), store: 64 (over y_hi, z, core).
Axes of the slice: x: 4, y: 4 (y_hi: 2, y_lo: 2; y = y_hi * 2 + y_lo), z: 16, core: 2. Of those that a mesh axis runs over, the one named last changes fastest.
Arguments:
- token_factors: float32 [8, 8192, 128], P('module', 'store'), may hold values from -4 to 4
- query_tokens: int32 [64, 8], P('store'), may hold values from 1 to 64, 128 in all within a row
- fisher_inverse: float32 [8, 4096, 4096], P('module', 'store'), may hold values from -0.09375 to 0.09375
- train_grads: bfloat16 [8, 24576, 4096], P('module', 'store'), may hold values from -0.09375 to 0.09375
Outputs:
- scores: float32 [24576, 512], P('store', 'module')
Inputs may be any that keep to these rules, and one draw needn't show every extreme that they name: `query_tokens`: each row (the queries of one index of store) holds 8 counts of at least 1 that sum to 128; in every row the largest count is exactly 64.
All inputs are finite; a program needn't handle non-finite values.
Results may differ from a plain program's by a relative error of at most 0.0029.
Values may be sent and summed in bfloat16 or wider, within the bound.
No kernel may reach another device: no remote copies, remote signals or barrier semaphores. Data moves between devices by JAX's collectives and lax.ppermute only.
A program may use at most 64 MiB of HBM per device.

v0:
```python
import jax
import jax.numpy as jnp
from jax import lax
from jax.sharding import PartitionSpec as P


def grads_of(factors, counts):
    width = factors.shape[1] // 2
    ends = jnp.cumsum(counts)
    starts = ends - counts
    position = jnp.arange(factors.shape[0], dtype=jnp.int32)
    owner = ((position[:, None] >= starts[None, :]) & (position[:, None] < ends[None, :])).astype(
        jnp.float32
    )
    inputs = factors[:, :width]
    outgrad = factors[:, width:]
    weighted = (owner[:, :, None] * outgrad[:, None, :]).reshape(
        factors.shape[0], counts.shape[0] * width
    )
    grads = lax.dot_general(
        weighted,
        inputs,
        (((0,), (0,)), ((), ())),
        precision=lax.Precision.HIGHEST,
        preferred_element_type=jnp.float32,
    )
    return grads.reshape(counts.shape[0], width * width)


def body(token_factors, query_tokens, fisher_inverse, train_grads):
    factors = token_factors[0]
    fisher_rows = fisher_inverse[0]
    stored = train_grads[0]
    local_grads = grads_of(factors, query_tokens[0])
    conditioned = lax.dot_general(
        lax.all_gather(local_grads, "store", axis=0, tiled=True),
        fisher_rows,
        (((1,), (1,)), ((), ())),
        precision=lax.Precision.HIGHEST,
        preferred_element_type=jnp.float32,
    )
    conditioned = conditioned.astype(jnp.bfloat16)
    module_scores = lax.dot_general(
        stored,
        lax.all_gather(conditioned, "store", axis=1, tiled=True),
        (((1,), (1,)), ((), ())),
        preferred_element_type=jnp.float32,
    )
    return lax.psum_scatter(module_scores, "module", scatter_dimension=1, tiled=True)


def solution(mesh):
    return jax.shard_map(
        body,
        mesh=mesh,
        in_specs=(
            P("module", "store", None),
            P("store", None),
            P("module", "store", None),
            P("module", "store", None),
        ),
        out_specs=P("store", "module"),
        check_vma=False,
    )
```

profile of v0, /device:TPU:1, one launch (start us, length us, event | category | flops | bytes accessed | tf_op | source)
XLA Modules:
  0.0 387.3 jit_solution(6891812257032974340)
XLA Ops:
  6.5 0.0 copy-start
  6.5 0.0 all-gather.3.cloned.1.call-start
  6.5 1.0 reduce-window.4
  7.5 0.7 fusion.10
  8.2 0.9 slice.8
  9.1 0.1 copy.7
  9.2 0.1 fusion.9
  9.3 1.2 fusion.6
  10.5 0.8 reshape.61
  11.3 0.0 all-gather.3.cloned.1.call-update
  11.3 0.0 all-gather.5.cloned.1.call-start
  11.3 170.9 %all-gather.3.cloned.1.call-done = f32[512,4096]{1,0:T(8,128)} async-done(((f32[8,4096]{1,0:T(8,128)}), f32[512,4096]{1,0:T(8,128)}) %all-gather.3.cloned.1.call-update) | async-done | bytes 8388624 | tf_op jit(solution)/shard_map/all_gather | solution.py:36
  182.2 12.4 %convolution_convert_fusion = bf16[512,64]{0,1:T(8,128)(2,1)} fusion(f32[512,4096]{1,0:T(8,128)} %all-gather.3.cloned.1.call-done, f32[1,64,4096]{2,1,0:T(8,128)} %param.6), kind=kOutput, calls=%fused_computation.3 | convolution fusion | flops 1610645504 | bytes 9502720 | tf_op jit(solution)/shard_map/dot_general | solution.py:35
  194.6 0.0 all-gather.5.cloned.1.call-update
  194.6 0.0 reduce-scatter.2.cloned.1.call-start
  194.7 145.3 %all-gather.5.cloned.1.call-done = bf16[512,4096]{0,1:T(8,128)(2,1)} async-done(((bf16[512,64]{0,1:T(8,128)(2,1)}), bf16[512,4096]{0,1:T(8,128)(2,1)}) %all-gather.5.cloned.1.call-update) | async-done | bytes 4194320 | tf_op jit(solution)/shard_map/all_gather | solution.py:45
  340.0 0.0 copy-done
  340.0 5.5 %fusion.2 = f32[384,512]{0,1:T(8,128)} fusion(bf16[512,4096]{0,1:T(8,128)(2,1)} %all-gather.5.cloned.1.call-done, bf16[1,384,4096]{2,1,0:T(8,128)(2,1)S(1)} %copy-done), kind=kOutput, calls=%fused_computation.2 | convolution fusion | flops 1610612736 | bytes 8126464 | tf_op jit(solution)/shard_map/dot_general | solution.py:43
  345.5 0.0 reduce-scatter.2.cloned.1.call-update
  345.5 35.3 %reduce-scatter.2.cloned.1.call-done = f32[384,64]{0,1:T(8,128)} async-done(((f32[384,512]{0,1:T(8,128)}), f32[384,64]{0,1:T(8,128)}) %reduce-scatter.2.cloned.1.call-update) | async-done | bytes 98320 | tf_op jit(solution)/shard_map/reduce_scatter | solution.py:49
  (1 shorter events, 0.0 us)
Async XLA Ops:
  6.5 333.5 %copy-start = (bf16[1,384,4096]{2,1,0:T(8,128)(2,1)S(1)}, bf16[1,384,4096]{2,1,0:T(8,128)(2,1)}, u32[]{:S(2)}) copy-start(bf16[1,384,4096]{2,1,0:T(8,128)(2,1)} %param.7) | copy-start | bytes 9437188
  6.5 175.7 %all-gather.3.cloned.1.call-start = ((), (), s32[]{:S(2)}) async-start(), calls=%async_computation.1 | async-start | bytes 8519680 | tf_op jit(solution)/shard_map/all_gather | solution.py:36
  11.3 328.7 %all-gather.5.cloned.1.call-start = ((), (), s32[]{:S(2)}) async-start(), calls=%async_computation.2 | async-start | bytes 4259840 | tf_op jit(solution)/shard_map/all_gather | solution.py:45
  194.6 186.2 %reduce-scatter.2.cloned.1.call-start = ((), (), s32[]{:S(2)}) async-start(), calls=%async_computation.3 | async-start | bytes 884736 | tf_op jit(solution)/shard_map/reduce_scatter | solution.py:49
Sparse Core Ops, SparseCore 0:
  11.4 170.7 all-gather.2
  194.7 145.2 all-gather.4
  345.6 35.1 reduce-scatter.1
where the time goes:
time: 392 us; the launch traced here: 387 us
  waiting for transfers between devices  352 us (90%)
  matrix products  19 us (5%)
  between operations  13.1 us (3%)
    all_gather x1, waiting for transfers between devices, body(): lax.all_gather(local_grads, 'store', axis=0, tiled=True)  171 us
    all_gather x1, waiting for transfers between devices, body(): lax.all_gather(conditioned, 'store', axis=1, tiled=True)  145 us
    reduce_scatter x1, waiting for transfers between devices, body(): lax.psum_scatter(module_scores, 'module', scatter_dimension=1, tiled=True)  35.3 us
    dot_general x1, matrix products, body(): lax.dot_general(lax.all_gather(local_grads, 'store', axis=0, tiled=True),...  12.4 us
  transfers between devices with their start and end apart: 3, of which 3 were waited for; matrix products, arithmetic and copies ran while one was open for 0% of the time, Pallas kernels for 0%

commit v1 on v0

v1 whole, which is shorter than its diff:
```python
import functools

import jax
import jax.numpy as jnp
from jax import lax
from jax.experimental import pallas as pl
from jax.experimental.pallas import tpu as pltpu
from jax.sharding import Mesh, PartitionSpec as P

AXES = ("x", "yl", "yh", "z", "c")
F32, BF16, I32, I16 = jnp.float32, jnp.bfloat16, jnp.int32, jnp.int16
NT = (((1,), (1,)), ((), ()))
VMEM = pltpu.VMEM


def exponent(largest):
    return jnp.floor(jnp.log2(jnp.maximum(largest, 1e-30))) - 13.0


def coded(x, k):
    return jnp.round(x * jnp.exp2(-k)).astype(I32).astype(I16)


def split(x):
    hi = x.astype(BF16)
    return hi, (x - hi.astype(F32)).astype(BF16)


def encode_kernel(counts_ref, tok_ref, out_ref, buf):
    buf[...] = tok_ref[...].T
    rank = buf.shape[0] // 2
    ins = buf[:rank, :]
    ogs = buf[rank:, :]
    k_in = exponent(jnp.max(jnp.abs(ins), axis=0, keepdims=True))
    k_og = exponent(jnp.max(jnp.abs(ogs), axis=0, keepdims=True))
    t = lax.broadcasted_iota(I32, (1, buf.shape[1]), 1)
    owner = jnp.zeros_like(t)
    end = 0
    for j in range(7):
        end = end + counts_ref[0, j]
        owner = owner + (t >= end).astype(I32)
    even = buf[pl.ds(rank, rank // 2, stride=2), :]
    odd = buf[pl.ds(rank + 1, rank // 2, stride=2), :]
    row = lax.broadcasted_iota(I32, (8, buf.shape[1]), 0)
    extra = jnp.where(row == 0, k_in, jnp.where(row == 1, k_og, owner.astype(F32)))
    out_ref[:rank, :] = coded(ins, k_in)
    out_ref[rank : rank + rank // 2, :] = coded(even, k_og)
    out_ref[rank + rank // 2 : 2 * rank, :] = coded(odd, k_og)
    out_ref[2 * rank :, :] = extra.astype(I32).astype(I16)


def condition_kernel(tok_ref, mine_ref, other_ref, out_ref, g_hi, g_lo, f_hi, f_lo):
    nz = tok_ref.shape[0]
    core = lax.axis_index("c")
    for ref, at in ((mine_ref, core), (other_ref, 1 - core)):
        rows = ref.shape[0]
        hi, lo = split(ref[...])
        at = pl.multiple_of(at * rows, rows)
        f_hi[pl.ds(at, rows), :] = hi
        f_lo[pl.ds(at, rows), :] = lo

    def block(z, yh):
        x = tok_ref[z, yh].astype(I32).astype(F32)
        s_in = jnp.exp2(x[128:129, :])
        s_og = jnp.exp2(x[129:130, :])
        owner = x[130:131, :]
        j = lax.broadcasted_iota(I32, (8, 128), 0).astype(F32)
        mask = jnp.where(owner == j, 1.0, 0.0)
        in_hi, in_lo = split(x[0:64, :] * s_in)
        zero = jnp.zeros((64, 128), BF16)

        def diagonal(v):
            return jnp.concatenate(
                [jnp.concatenate([v, zero], axis=1), jnp.concatenate([zero, v], axis=1)], axis=0
            )

        r_hi, r_lo = diagonal(in_hi), diagonal(in_lo)

        def spread(v):
            w = v * s_og
            hi = w.astype(BF16).astype(F32)
            lo = w - hi
            return [
                (u[:, None, :] * mask[None]).reshape(256, 128).astype(BF16) for u in (hi, lo)
            ]

        e_hi, e_lo = spread(x[64:96, :])
        o_hi, o_lo = spread(x[96:128, :])
        l_hi = jnp.concatenate([e_hi, o_hi], axis=1)
        l_lo = jnp.concatenate([e_lo, o_lo], axis=1)
        two = lax.dot_general(
            l_hi, jnp.concatenate([r_hi, r_lo], axis=0), NT, preferred_element_type=F32
        )
        one = lax.dot_general(l_lo, r_hi, NT, preferred_element_type=F32)
        return (two[:, :128] + two[:, 128:] + one).reshape(32, 8, 128)

    def step(s, carry):
        yh = s // (nz // 2)
        z = (s % (nz // 2)) * 2
        g = jnp.concatenate([block(z, yh), block(z + 1, yh)], axis=1)
        hi, lo = split(g)
        at = pl.multiple_of(s * 16, 16)
        for a in range(32):
            g_hi[pl.ds(at, 16), a * 128 : (a + 1) * 128] = hi[a]
            g_lo[pl.ds(at, 16), a * 128 : (a + 1) * 128] = lo[a]
        return carry

    lax.fori_loop(0, nz, step, 0)
    dot = functools.partial(lax.dot_general, dimension_numbers=NT, preferred_element_type=F32)
    p = dot(g_hi[...], f_hi[...]) + dot(g_lo[...], f_hi[...]) + dot(g_hi[...], f_lo[...])
    k = exponent(jnp.max(jnp.abs(p), axis=0, keepdims=True))
    rows = p.shape[0]
    out_ref[:rows, :] = coded(p, k)
    out_ref[rows:, :] = jnp.broadcast_to(k, (8, 128)).astype(I32).astype(I16)


def score_kernel(p_ref, t_ref, swapped_ref, out_ref, p_all, t_own, sem):
    nz = p_ref.shape[0]
    half = t_own.shape[1]
    yh = lax.axis_index("yh")
    copy = pltpu.make_async_copy(
        t_ref.at[:, pl.ds(pl.multiple_of(yh * half, half), half)], t_own, sem
    )
    copy.start()
    for z in range(nz):
        parts = []
        for c in range(2):
            v = p_ref[z, c].astype(I32).astype(F32)
            parts.append((v[:256, :] * jnp.exp2(v[256:257, :])).reshape(32, 8, 128))
        p_all[:, z * 128 : (z + 1) * 128] = (
            jnp.concatenate(parts, axis=1).reshape(512, 128).astype(BF16)
        )
    copy.wait()
    for ref, at in ((t_own, yh), (swapped_ref, 1 - yh)):
        s = lax.dot_general(p_all[...], ref[...], NT, preferred_element_type=F32).astype(BF16)
        for m in range(8):
            out_ref[m, at] = s[m * 64 : (m + 1) * 64, :]


def swap(x, axis):
    return lax.ppermute(x, axis, [(0, 1), (1, 0)])


def body(token_factors, query_tokens, fisher_inverse, train_grads):
    fisher = fisher_inverse[0]
    stored = train_grads[0]
    examples, grad = stored.shape
    half = grad // 2
    vm = pl.BlockSpec(memory_space=VMEM)

    tokens = pl.pallas_call(
        encode_kernel,
        out_shape=jax.ShapeDtypeStruct((136, 128), I16),
        in_specs=[pl.BlockSpec(memory_space=pltpu.SMEM), vm],
        out_specs=vm,
        scratch_shapes=[VMEM((128, 128), F32)],
    )(query_tokens, token_factors[0])
    tokens = lax.all_gather(tokens, "yh")
    yh = lax.axis_index("yh")
    swapped = swap(lax.dynamic_slice_in_dim(stored, (1 - yh) * half, half, 1), "yh")
    fisher_other = swap(fisher, "c")
    tokens = lax.all_gather(tokens, "z")

    conditioned = pl.pallas_call(
        condition_kernel,
        out_shape=jax.ShapeDtypeStruct((264, 128), I16),
        in_specs=[vm, vm, vm],
        out_specs=vm,
        scratch_shapes=[VMEM((256, grad), BF16)] * 2 + [VMEM((128, grad), BF16)] * 2,
    )(tokens, fisher, fisher_other)
    conditioned = lax.all_gather(conditioned, ("z", "c")).reshape(16, 2, 264, 128)

    partial = pl.pallas_call(
        score_kernel,
        out_shape=jax.ShapeDtypeStruct((8, 2, 64, examples), BF16),
        in_specs=[vm, pl.BlockSpec(memory_space=pl.ANY), vm],
        out_specs=vm,
        scratch_shapes=[
            VMEM((512, half), BF16),
            VMEM((examples, half), BF16),
            pltpu.SemaphoreType.DMA,
        ],
    )(conditioned, stored, swapped)
    partial = lax.all_to_all(
        partial.reshape(16, 64, examples), ("x", "yl", "yh"), 0, 0, tiled=True
    )
    return jnp.sum(partial.astype(F32), axis=0).T


def solution(mesh):
    fine = Mesh(mesh.devices.reshape(4, 2, 2, 16, 2), AXES)
    module, store = ("x", "yl"), ("yh", "z", "c")
    return jax.shard_map(
        body,
        mesh=fine,
        in_specs=(
            P(module, store, None),
            P(store, None),
            P(module, store, None),
            P(module, store, None),
        ),
        out_specs=P(store, module),
        check_vma=False,
    )
```

time: 392 us -> 166 us (0.42); the launches traced: 387 us -> 165 us
  waiting for transfers between devices: 352 us -> 0.01 us
  blocking collectives: 0 us -> 133 us
  matrix products: 19 us -> 0 us
  Pallas kernels: 0 us -> 18.5 us
  between operations: 13.1 us -> 0.04 us
  starting transfers between devices: 0.09 us -> 10.7 us
    all_gather x2 -> x0, waiting for transfers between devices: 316 us -> none  [the longest x1 171 us: body(): lax.all_gather(local_grads, 'store', axis=0, tiled=True)]
    all_gather x0 -> x3, blocking collectives: none -> 112 us  [the longest x1 43.2 us: body(): lax.all_gather(conditioned, ('z', 'c')).reshape(16, 2, 264, 128)]
    reduce_scatter x1 -> x0, waiting for transfers between devices: 35.3 us -> none  [body(): lax.psum_scatter(module_scores, 'module', scatter_dimension=1, tiled=True)]
    all_to_all x0 -> x1, blocking collectives: none -> 20.5 us  [body(): lax.all_to_all(partial.reshape(16, 64, examples), ('x', 'yl', 'yh'), 0, 0...]
    dot_general x3 -> x0, matrix products: 19 us -> none  [the longest x1 12.4 us: body(): lax.dot_general(lax.all_gather(local_grads, 'store', axis=0, tiled=True),...]
    pallas_call x0 -> x3, Pallas kernels: none -> 18.5 us  [the longest x1 10.2 us: body(): pl.pallas_call(condition_kernel, out_shape=jax.ShapeDtypeStruct((264, 128...]
    ppermute x0 -> x2, starting transfers between devices: none -> 10.7 us  [swap(): return lax.ppermute(x, axis, [(0, 1), (1, 0)])]
  transfers between devices with their start and end apart: 3 -> 2, of which waited for: 3 -> 0; matrix products, arithmetic and copies ran while one was open for 0% -> 1% of each run, Pallas kernels for 0% -> 7%
where the time goes in v1:
time: 166 us; the launch traced here: 165 us
  blocking collectives  133 us (80%)
  Pallas kernels  18.5 us (11%)
  starting transfers between devices  10.7 us (6%)
  local copies, waits for them, and re-layouts  2.66 us (2%)
    all_gather x1, blocking collectives, body(): lax.all_gather(conditioned, ('z', 'c')).reshape(16, 2, 264, 128)  43.2 us
    all_gather x1, blocking collectives, body(): tokens = lax.all_gather(tokens, 'yh')  36.6 us
    all_gather x1, blocking collectives, body(): tokens = lax.all_gather(tokens, 'z')  32.5 us
    all_to_all x1, blocking collectives, body(): lax.all_to_all(partial.reshape(16, 64, examples), ('x', 'yl', 'yh'), 0, 0...  20.5 us
    ppermute x2, starting transfers between devices, swap(): return lax.ppermute(x, axis, [(0, 1), (1, 0)])  10.7 us
    pallas_call x1, Pallas kernels, body(): pl.pallas_call(condition_kernel, out_shape=jax.ShapeDtypeStruct((264, 128...  10.2 us
    pallas_call x1, Pallas kernels, body(): pl.pallas_call(score_kernel, out_shape=jax.ShapeDtypeStruct((8, 2, 64, ex...  6.7 us
  transfers between devices with their start and end apart: 2, of which 0 were waited for; matrix products, arithmetic and copies ran while one was open for 1% of the time, Pallas kernels for 7%

profile of v1, /device:TPU:1, one launch (start us, length us, event | category | flops | bytes accessed | tf_op | source)
XLA Modules:
  0.0 165.4 jit_solution(2227860857907387611)
XLA Ops:
  0.0 8.7 %collective-permute-start = (f32[64,4096]{1,0:T(8,128)}, f32[64,4096]{1,0:T(8,128)}, u32[]{:S(2)}, u32[]{:S(2)}) collective-permute-start(f32[64,4096]{1,0:T(8,128)} %bitcast.14), channel_id=1, source_target_pairs={{0,1},{1,0},{2,3},{3,2},{4,5},{5,4},{6,7},{7,6},{8,9},{9,8},{10,11... | collective-permute-start | bytes 3145736 | tf_op jit(solution)/shard_map/ppermute | solution.py:141
  8.8 1.5 dynamic-slice_bitcast_fusion
  10.3 1.9 %collective-permute-start.1 = (bf16[384,2048]{1,0:T(8,128)(2,1)S(1)}, bf16[384,2048]{1,0:T(8,128)(2,1)S(1)}, u32[]{:S(2)}, u32[]{:S(2)}) collective-permute-start(bf16[384,2048]{1,0:T(8,128)(2,1)S(1)} %dynamic-slice_bitcast_fusion), channel_id=1, source_target_pairs={{0,32},{32,0},{1,33},{33,1},{2,34},{34,2},{3,35},{35,3},{4,36},{36... | collective-permute-start | bytes 4718600 | tf_op jit(solution)/shard_map/ppermute | solution.py:141
  12.2 1.6 shard_map.46
  13.8 36.6 %all-gather = s16[272,128]{1,0:T(8,128)(2,1)S(1)} all-gather(s16[136,128]{1,0:T(8,128)(2,1)} %shard_map.46), channel_id=2, replica_groups=mesh['x'=4,'yl'=2,'yh'=2,'z'=16,'c'=2] {'yh'}, dimensions={0}, use_global_device_ids=true | all-gather | bytes 104448 | tf_op jit(solution)/shard_map/all_gather | solution.py:158
  50.4 32.5 %all-gather.5 = s16[32,136,128]{2,1,0:T(8,128)(2,1)} all-gather(s16[2,136,128]{2,1,0:T(8,128)(2,1)S(1)} %bitcast.16), channel_id=3, replica_groups=mesh['x'=4,'yl'=2,'yh'=2,'z'=16,'c'=2] {'z'}, dimensions={0}, use_global_device_ids=true | all-gather | bytes 1183744 | tf_op jit(solution)/shard_map/all_gather | solution.py:162
  82.9 0.0 collective-permute-done.other_ref
  82.9 10.2 %shard_map.47 = s16[264,128]{1,0:T(8,128)(2,1)} custom-call(s16[16,2,136,128]{3,2,1,0:T(8,128)(2,1)} %bitcast.12, f32[64,4096]{1,0:T(8,128)} %bitcast.15, f32[64,4096]{1,0:T(8,128)} %collective-permute-done.other_ref), custom_call_target="tpu_custom_call" | custom-call | tf_op jit(solution)/shard_map/pallas_call | solution.py:164
  93.1 43.2 %all-gather.6 = s16[8448,128]{1,0:T(8,128)(2,1)} all-gather(s16[264,128]{1,0:T(8,128)(2,1)} %shard_map.47), channel_id=4, replica_groups=mesh['x'=4,'yl'=2,'yh'=2,'z'=16,'c'=2] {'z','c'}, dimensions={0}, use_global_device_ids=true | all-gather | bytes 2230272 | tf_op jit(solution)/shard_map/all_gather | solution.py:171
  136.2 0.0 collective-permute-done.1.swapped_ref
  136.2 0.0 copy-start
  136.2 1.1 copy-done
  137.4 6.7 %shard_map.48 = bf16[8,2,64,384]{3,2,1,0:T(8,128)(2,1)} custom-call(s16[16,2,264,128]{3,2,1,0:T(8,128)(2,1)} %bitcast.10, bf16[384,4096]{1,0:T(8,128)(2,1)} %bitcast.11, bf16[384,2048]{1,0:T(8,128)(2,1)} %copy-done), custom_call_target="tpu_custom_call" | custom-call | tf_op jit(solution)/shard_map/pallas_call | solution.py:173
  144.1 20.5 %all_to_all.5 = bf16[16,64,384]{2,1,0:T(8,128)(2,1)S(1)} all-to-all(bf16[16,64,384]{2,1,0:T(8,128)(2,1)} %bitcast.13), channel_id=1, replica_groups=mesh['x'=4,'yl'=2,'yh'=2,'z'=16,'c'=2] {'x','yl','yh'}, dimensions={0} | all-to-all | bytes 1572864 | tf_op jit(solution)/shard_map/all_to_all | solution.py:184
  164.6 0.7 convert_reduce_fusion
Async XLA Ops:
  0.0 82.9 %collective-permute-start = (f32[64,4096]{1,0:T(8,128)}, f32[64,4096]{1,0:T(8,128)}, u32[]{:S(2)}, u32[]{:S(2)}) collective-permute-start(f32[64,4096]{1,0:T(8,128)} %bitcast.14), channel_id=1, source_target_pairs={{0,1},{1,0},{2,3},{3,2},{4,5},{5,4},{6,7},{7,6},{8,9},{9,8},{10,11... | collective-permute-start | bytes 3145736 | tf_op jit(solution)/shard_map/ppermute | solution.py:141
  10.3 126.0 %collective-permute-start.1 = (bf16[384,2048]{1,0:T(8,128)(2,1)S(1)}, bf16[384,2048]{1,0:T(8,128)(2,1)S(1)}, u32[]{:S(2)}, u32[]{:S(2)}) collective-permute-start(bf16[384,2048]{1,0:T(8,128)(2,1)S(1)} %dynamic-slice_bitcast_fusion), channel_id=1, source_target_pairs={{0,32},{32,0},{1,33},{33,1},{2,34},{34,2},{3,35},{35,3},{4,36},{36... | collective-permute-start | bytes 4718600 | tf_op jit(solution)/shard_map/ppermute | solution.py:141
  136.2 1.1 copy-start

commit v2 on v1

--- a/solution.py
+++ b/solution.py
@@ -26,7 +26,11 @@
     return hi, (x - hi.astype(F32)).astype(BF16)
 
 
-def encode_kernel(counts_ref, tok_ref, out_ref, buf):
+def encode_kernel(counts_ref, tok_ref, t_ref, out_ref, half_ref, buf, sem):
+    half = half_ref.shape[1]
+    at = pl.multiple_of((1 - lax.axis_index("yh")) * half, half)
+    copy = pltpu.make_async_copy(t_ref.at[:, pl.ds(at, half)], half_ref, sem)
+    copy.start()
     buf[...] = tok_ref[...].T
     rank = buf.shape[0] // 2
     ins = buf[:rank, :]
@@ -47,6 +51,7 @@
     out_ref[rank : rank + rank // 2, :] = coded(even, k_og)
     out_ref[rank + rank // 2 : 2 * rank, :] = coded(odd, k_og)
     out_ref[2 * rank :, :] = extra.astype(I32).astype(I16)
+    copy.wait()
 
 
 def condition_kernel(tok_ref, mine_ref, other_ref, out_ref, g_hi, g_lo, f_hi, f_lo):
@@ -114,14 +119,10 @@
     out_ref[rows:, :] = jnp.broadcast_to(k, (8, 128)).astype(I32).astype(I16)
 
 
-def score_kernel(p_ref, t_ref, swapped_ref, out_ref, p_all, t_own, sem):
+def score_kernel(p_ref, t_ref, swapped_ref, out_ref, p_all):
     nz = p_ref.shape[0]
-    half = t_own.shape[1]
+    half = swapped_ref.shape[1]
     yh = lax.axis_index("yh")
-    copy = pltpu.make_async_copy(
-        t_ref.at[:, pl.ds(pl.multiple_of(yh * half, half), half)], t_own, sem
-    )
-    copy.start()
     for z in range(nz):
         parts = []
         for c in range(2):
@@ -130,11 +131,15 @@
         p_all[:, z * 128 : (z + 1) * 128] = (
             jnp.concatenate(parts, axis=1).reshape(512, 128).astype(BF16)
         )
-    copy.wait()
-    for ref, at in ((t_own, yh), (swapped_ref, 1 - yh)):
-        s = lax.dot_general(p_all[...], ref[...], NT, preferred_element_type=F32).astype(BF16)
+    own = t_ref[:, pl.ds(pl.multiple_of(yh * half, half), half)]
+    for t, at in ((own, yh), (swapped_ref[...], 1 - yh)):
+        s = lax.dot_general(p_all[...], t, NT, preferred_element_type=F32).astype(BF16)
         for m in range(8):
             out_ref[m, at] = s[m * 64 : (m + 1) * 64, :]
+
+
+def grant(mib):
+    return pltpu.CompilerParams(vmem_limit_bytes=mib << 20)
 
 
 def swap(x, axis):
@@ -148,16 +153,24 @@
     half = grad // 2
     vm = pl.BlockSpec(memory_space=VMEM)
 
-    tokens = pl.pallas_call(
+    tokens, swapped = pl.pallas_call(
         encode_kernel,
-        out_shape=jax.ShapeDtypeStruct((136, 128), I16),
-        in_specs=[pl.BlockSpec(memory_space=pltpu.SMEM), vm],
-        out_specs=vm,
-        scratch_shapes=[VMEM((128, 128), F32)],
-    )(query_tokens, token_factors[0])
+        out_shape=(
+            jax.ShapeDtypeStruct((136, 128), I16),
+            jax.ShapeDtypeStruct((examples, half), BF16),
+        ),
+        in_specs=[
+            pl.BlockSpec(memory_space=pltpu.SMEM),
+            vm,
+            pl.BlockSpec(memory_space=pl.ANY),
+        ],
+        out_specs=(vm, vm),
+        scratch_shapes=[VMEM((128, 128), F32), pltpu.SemaphoreType.DMA],
+        compiler_params=grant(60),
+    )(query_tokens, token_factors[0], stored)
     tokens = lax.all_gather(tokens, "yh")
-    yh = lax.axis_index("yh")
-    swapped = swap(lax.dynamic_slice_in_dim(stored, (1 - yh) * half, half, 1), "yh")
+    tokens, swapped, fisher = lax.optimization_barrier((tokens, swapped, fisher))
+    swapped = swap(swapped, "yh")
     fisher_other = swap(fisher, "c")
     tokens = lax.all_gather(tokens, "z")
 
@@ -167,19 +180,17 @@
         in_specs=[vm, vm, vm],
         out_specs=vm,
         scratch_shapes=[VMEM((256, grad), BF16)] * 2 + [VMEM((128, grad), BF16)] * 2,
+        compiler_params=grant(24),
     )(tokens, fisher, fisher_other)
     conditioned = lax.all_gather(conditioned, ("z", "c")).reshape(16, 2, 264, 128)
 
     partial = pl.pallas_call(
         score_kernel,
         out_shape=jax.ShapeDtypeStruct((8, 2, 64, examples), BF16),
-        in_specs=[vm, pl.BlockSpec(memory_space=pl.ANY), vm],
+        in_specs=[vm, vm, vm],
         out_specs=vm,
-        scratch_shapes=[
-            VMEM((512, half), BF16),
-            VMEM((examples, half), BF16),
-            pltpu.SemaphoreType.DMA,
-        ],
+        scratch_shapes=[VMEM((512, half), BF16)],
+        compiler_params=grant(24),
     )(conditioned, stored, swapped)
     partial = lax.all_to_all(
         partial.reshape(16, 64, examples), ("x", "yl", "yh"), 0, 0, tiled=True

time: 166 us -> 123 us (0.74)
  blocking collectives: 133 us -> 97.8 us
  Pallas kernels: 18.5 us -> 13.6 us
  local copies, waits for them, and re-layouts: 2.66 us -> 0.01 us
    all_gather x1, blocking collectives: 36.6 us -> 5.99 us  [body(): tokens = lax.all_gather(tokens, 'yh')]
    all_gather x1, blocking collectives: 43.2 us -> 38.7 us  [body(): lax.all_gather(conditioned, ('z', 'c')).reshape(16, 2, 264, 128)]
    pallas_call x1, Pallas kernels: 6.7 us -> 2.36 us  [body(): pl.pallas_call(score_kernel, out_shape=jax.ShapeDtypeStruct((8, 2, 64, ex...]
    pallas_call x1, Pallas kernels: 10.2 us -> 7.71 us  [body(): pl.pallas_call(condition_kernel, out_shape=jax.ShapeDtypeStruct((264, 128...]
    all_gather x1, blocking collectives: 32.5 us -> 34.9 us  [body(): tokens = lax.all_gather(tokens, 'z')]
    all_to_all x1, blocking collectives: 20.5 us -> 18.2 us  [body(): lax.all_to_all(partial.reshape(16, 64, examples), ('x', 'yl', 'yh'), 0, 0...]
    pallas_call x1, Pallas kernels: 1.6 us -> 3.55 us  [body(): pl.pallas_call(encode_kernel, out_shape=(jax.ShapeDtypeStruct((136, 128),...]
  transfers between devices with their start and end apart: 2 -> 2, of which waited for: 0 -> 0; matrix products, arithmetic and copies ran while one was open for 1% -> 0% of each run, Pallas kernels for 7% -> 6%
where the time goes in v2:
time: 123 us
  blocking collectives  97.8 us (80%)
  Pallas kernels  13.6 us (11%)
  starting transfers between devices  11 us (9%)
    all_gather x1, blocking collectives, body(): lax.all_gather(conditioned, ('z', 'c')).reshape(16, 2, 264, 128)  38.7 us
    all_gather x1, blocking collectives, body(): tokens = lax.all_gather(tokens, 'z')  34.9 us
    all_to_all x1, blocking collectives, body(): lax.all_to_all(partial.reshape(16, 64, examples), ('x', 'yl', 'yh'), 0, 0...  18.2 us
    ppermute x2, starting transfers between devices, swap(): return lax.ppermute(x, axis, [(0, 1), (1, 0)])  11 us
    pallas_call x1, Pallas kernels, body(): pl.pallas_call(condition_kernel, out_shape=jax.ShapeDtypeStruct((264, 128...  7.71 us
    all_gather x1, blocking collectives, body(): tokens = lax.all_gather(tokens, 'yh')  5.99 us
    pallas_call x1, Pallas kernels, body(): pl.pallas_call(encode_kernel, out_shape=(jax.ShapeDtypeStruct((136, 128),...  3.55 us
  transfers between devices with their start and end apart: 2, of which 0 were waited for; matrix products, arithmetic and copies ran while one was open for 0% of the time, Pallas kernels for 6%

profile of v2, /device:TPU:1, one launch (start us, length us, event | category | flops | bytes accessed | tf_op | source)
XLA Modules:
  0.0 123.2 jit_solution(1196094701989187184)
XLA Ops:
  0.0 0.0 copy-start.1
  0.0 3.5 %shard_map.46 = (s16[136,128]{1,0:T(8,128)(2,1)}, bf16[384,2048]{1,0:T(8,128)(2,1)}) custom-call(s32[1,8]{1,0:T(1,128)} %counts_ref.1, f32[128,128]{1,0:T(8,128)} %bitcast.16, bf16[384,4096]{1,0:T(8,128)(2,1)} %bitcast.8), custom_call_target="tpu_custom_call" | custom-call | tf_op jit(solution)/shard_map/pallas_call | solution.py:156
  3.6 6.0 %all-gather = s16[272,128]{1,0:T(8,128)(2,1)S(1)} all-gather(s16[136,128]{1,0:T(8,128)(2,1)} %get-tuple-element.10), channel_id=2, replica_groups=mesh['x'=4,'yl'=2,'yh'=2,'z'=16,'c'=2] {'yh'}, dimensions={0}, use_global_device_ids=true | all-gather | bytes 104448 | tf_op jit(solution)/shard_map/all_gather | solution.py:171
  9.5 0.0 copy-done.1
  9.5 9.1 %collective-permute-start = (f32[64,4096]{1,0:T(8,128)S(1)}, f32[64,4096]{1,0:T(8,128)S(1)}, u32[]{:S(2)}, u32[]{:S(2)}) collective-permute-start(f32[64,4096]{1,0:T(8,128)S(1)} %bitcast.13), channel_id=1, source_target_pairs={{0,1},{1,0},{2,3},{3,2},{4,5},{5,4},{6,7},{7,6},{8,9},{9,8},{10,11... | collective-permute-start | bytes 3145736 | tf_op jit(solution)/shard_map/ppermute | solution.py:146
  18.6 1.9 %collective-permute-start.1 = (bf16[384,2048]{1,0:T(8,128)(2,1)}, bf16[384,2048]{1,0:T(8,128)(2,1)S(1)}, u32[]{:S(2)}, u32[]{:S(2)}) collective-permute-start(bf16[384,2048]{1,0:T(8,128)(2,1)} %get-tuple-element.14), channel_id=1, source_target_pairs={{0,32},{32,0},{1,33},{33,1},{2,34},{34,2},{3,35},{35,3},{4,36},{36... | collective-permute-start | bytes 4718600 | tf_op jit(solution)/shard_map/ppermute | solution.py:146
  20.6 34.9 %all-gather.5 = s16[32,136,128]{2,1,0:T(8,128)(2,1)S(1)} all-gather(s16[2,136,128]{2,1,0:T(8,128)(2,1)S(1)} %bitcast.15), channel_id=3, replica_groups=mesh['x'=4,'yl'=2,'yh'=2,'z'=16,'c'=2] {'z'}, dimensions={0}, use_global_device_ids=true | all-gather | bytes 1183744 | tf_op jit(solution)/shard_map/all_gather | solution.py:175
  55.5 0.0 collective-permute-done.other_ref
  55.5 0.0 copy-start
  55.5 7.7 %shard_map.47 = s16[264,128]{1,0:T(8,128)(2,1)S(1)} custom-call(s16[16,2,136,128]{3,2,1,0:T(8,128)(2,1)S(1)} %bitcast.11, f32[64,4096]{1,0:T(8,128)S(1)} %bitcast.14, f32[64,4096]{1,0:T(8,128)S(1)} %collective-permute-done.other_ref), custom_call_target="tpu_custom_call" | custom-call | tf_op jit(solution)/shard_map/pallas_call | solution.py:177
  63.2 38.7 %all-gather.6 = s16[8448,128]{1,0:T(8,128)(2,1)S(1)} all-gather(s16[264,128]{1,0:T(8,128)(2,1)S(1)} %shard_map.47), channel_id=4, replica_groups=mesh['x'=4,'yl'=2,'yh'=2,'z'=16,'c'=2] {'z','c'}, dimensions={0}, use_global_device_ids=true | all-gather | bytes 2230272 | tf_op jit(solution)/shard_map/all_gather | solution.py:185
  101.9 0.0 collective-permute-done.1.swapped_ref
  101.9 0.0 copy-done
  101.9 2.4 %shard_map.48 = bf16[8,2,64,384]{3,2,1,0:T(8,128)(2,1)S(1)} custom-call(s16[16,2,264,128]{3,2,1,0:T(8,128)(2,1)S(1)} %bitcast.10, bf16[384,4096]{1,0:T(8,128)(2,1)S(1)} %bitcast.9, bf16[384,2048]{1,0:T(8,128)(2,1)S(1)} %collective-permute-done.1.swapped_ref), custom_call_target="tpu_custom_call" | custom-call | tf_op jit(solution)/shard_map/pallas_call | solution.py:187
  104.3 18.2 %all_to_all.5 = bf16[16,64,384]{2,1,0:T(8,128)(2,1)S(1)} all-to-all(bf16[16,64,384]{2,1,0:T(8,128)(2,1)S(1)} %bitcast.12), channel_id=1, replica_groups=mesh['x'=4,'yl'=2,'yh'=2,'z'=16,'c'=2] {'x','yl','yh'}, dimensions={0} | all-to-all | bytes 1572864 | tf_op jit(solution)/shard_map/all_to_all | solution.py:195
  122.5 0.7 convert_reduce_fusion
Async XLA Ops:
  0.0 9.5 %copy-start.1 = (f32[1,64,4096]{2,1,0:T(8,128)S(1)}, f32[1,64,4096]{2,1,0:T(8,128)}, u32[]{:S(2)}) copy-start(f32[1,64,4096]{2,1,0:T(8,128)} %param.6) | copy-start | bytes 3145732
  9.5 46.0 %collective-permute-start = (f32[64,4096]{1,0:T(8,128)S(1)}, f32[64,4096]{1,0:T(8,128)S(1)}, u32[]{:S(2)}, u32[]{:S(2)}) collective-permute-start(f32[64,4096]{1,0:T(8,128)S(1)} %bitcast.13), channel_id=1, source_target_pairs={{0,1},{1,0},{2,3},{3,2},{4,5},{5,4},{6,7},{7,6},{8,9},{9,8},{10,11... | collective-permute-start | bytes 3145736 | tf_op jit(solution)/shard_map/ppermute | solution.py:146
  18.6 83.3 %collective-permute-start.1 = (bf16[384,2048]{1,0:T(8,128)(2,1)}, bf16[384,2048]{1,0:T(8,128)(2,1)S(1)}, u32[]{:S(2)}, u32[]{:S(2)}) collective-permute-start(bf16[384,2048]{1,0:T(8,128)(2,1)} %get-tuple-element.14), channel_id=1, source_target_pairs={{0,32},{32,0},{1,33},{33,1},{2,34},{34,2},{3,35},{35,3},{4,36},{36... | collective-permute-start | bytes 4718600 | tf_op jit(solution)/shard_map/ppermute | solution.py:146
  55.5 46.4 %copy-start = (bf16[1,384,4096]{2,1,0:T(8,128)(2,1)S(1)}, bf16[1,384,4096]{2,1,0:T(8,128)(2,1)}, u32[]{:S(2)}) copy-start(bf16[1,384,4096]{2,1,0:T(8,128)(2,1)} %param.7) | copy-start | bytes 9437188

commit v3 on v2

--- a/solution.py
+++ b/solution.py
@@ -11,6 +11,8 @@
 F32, BF16, I32, I16 = jnp.float32, jnp.bfloat16, jnp.int32, jnp.int16
 NT = (((1,), (1,)), ((), ()))
 VMEM = pltpu.VMEM
+UNROLL = 8
+CHUNKS = 6
 
 
 def exponent(largest):
@@ -26,11 +28,21 @@
     return hi, (x - hi.astype(F32)).astype(BF16)
 
 
-def encode_kernel(counts_ref, tok_ref, t_ref, out_ref, half_ref, buf, sem):
+def encode_kernel(counts_ref, tok_ref, t_ref, out_ref, half_ref, buf, rows, load, store):
     half = half_ref.shape[1]
     at = pl.multiple_of((1 - lax.axis_index("yh")) * half, half)
-    copy = pltpu.make_async_copy(t_ref.at[:, pl.ds(at, half)], half_ref, sem)
-    copy.start()
+    chunk = rows.shape[0] // CHUNKS
+    pieces = [pl.ds(i * chunk, chunk) for i in range(CHUNKS)]
+    loads = [
+        pltpu.make_async_copy(t_ref.at[piece, pl.ds(at, half)], rows.at[piece], load.at[i])
+        for i, piece in enumerate(pieces)
+    ]
+    stores = [
+        pltpu.make_async_copy(rows.at[piece], half_ref.at[piece], store.at[i])
+        for i, piece in enumerate(pieces)
+    ]
+    for copy in loads:
+        copy.start()
     buf[...] = tok_ref[...].T
     rank = buf.shape[0] // 2
     ins = buf[:rank, :]
@@ -39,6 +51,9 @@
     k_og = exponent(jnp.max(jnp.abs(ogs), axis=0, keepdims=True))
     t = lax.broadcasted_iota(I32, (1, buf.shape[1]), 1)
     owner = jnp.zeros_like(t)
+    for i in range(CHUNKS // 2):
+        loads[i].wait()
+        stores[i].start()
     end = 0
     for j in range(7):
         end = end + counts_ref[0, j]
@@ -51,27 +66,22 @@
     out_ref[rank : rank + rank // 2, :] = coded(even, k_og)
     out_ref[rank + rank // 2 : 2 * rank, :] = coded(odd, k_og)
     out_ref[2 * rank :, :] = extra.astype(I32).astype(I16)
-    copy.wait()
-
-
-def condition_kernel(tok_ref, mine_ref, other_ref, out_ref, g_hi, g_lo, f_hi, f_lo):
+    for i in range(CHUNKS // 2, CHUNKS):
+        loads[i].wait()
+        stores[i].start()
+    for copy in stores:
+        copy.wait()
+
+
+def condition_kernel(tok_ref, mine_ref, other_ref, out_ref, grads, wide):
     nz = tok_ref.shape[0]
     core = lax.axis_index("c")
-    for ref, at in ((mine_ref, core), (other_ref, 1 - core)):
-        rows = ref.shape[0]
-        hi, lo = split(ref[...])
-        at = pl.multiple_of(at * rows, rows)
-        f_hi[pl.ds(at, rows), :] = hi
-        f_lo[pl.ds(at, rows), :] = lo
-
-    def block(z, yh):
-        x = tok_ref[z, yh].astype(I32).astype(F32)
-        s_in = jnp.exp2(x[128:129, :])
-        s_og = jnp.exp2(x[129:130, :])
-        owner = x[130:131, :]
-        j = lax.broadcasted_iota(I32, (8, 128), 0).astype(F32)
-        mask = jnp.where(owner == j, 1.0, 0.0)
-        in_hi, in_lo = split(x[0:64, :] * s_in)
+    j = lax.broadcasted_iota(I32, (8, 128), 0).astype(F32)
+
+    def block(z, yh, slot):
+        x = tok_ref[z, core, yh].astype(I32).astype(F32)
+        mask = jnp.where(x[130:131, :] == j, 1.0, 0.0)
+        in_hi, in_lo = split(x[0:64, :] * jnp.exp2(x[128:129, :]))
         zero = jnp.zeros((64, 128), BF16)
 
         def diagonal(v):
@@ -80,39 +90,48 @@
             )
 
         r_hi, r_lo = diagonal(in_hi), diagonal(in_lo)
-
-        def spread(v):
-            w = v * s_og
-            hi = w.astype(BF16).astype(F32)
-            lo = w - hi
-            return [
-                (u[:, None, :] * mask[None]).reshape(256, 128).astype(BF16) for u in (hi, lo)
-            ]
-
-        e_hi, e_lo = spread(x[64:96, :])
-        o_hi, o_lo = spread(x[96:128, :])
-        l_hi = jnp.concatenate([e_hi, o_hi], axis=1)
-        l_lo = jnp.concatenate([e_lo, o_lo], axis=1)
+        w = x[64:128, :] * jnp.exp2(x[129:130, :])
+        hi = w.astype(BF16).astype(F32)
+        wide[slot, 0] = hi
+        wide[slot, 1] = w - hi
+
+        def spread(part):
+            halves = []
+            for odd in range(2):
+                rows = [
+                    wide[slot, part, pl.ds(odd * 32 + a, 8, stride=0), :] * mask
+                    for a in range(32)
+                ]
+                halves.append(jnp.concatenate(rows, axis=0).astype(BF16))
+            return jnp.concatenate(halves, axis=1)
+
         two = lax.dot_general(
-            l_hi, jnp.concatenate([r_hi, r_lo], axis=0), NT, preferred_element_type=F32
+            spread(0), jnp.concatenate([r_hi, r_lo], axis=0), NT, preferred_element_type=F32
         )
-        one = lax.dot_general(l_lo, r_hi, NT, preferred_element_type=F32)
-        return (two[:, :128] + two[:, 128:] + one).reshape(32, 8, 128)
+        one = lax.dot_general(spread(1), r_hi, NT, preferred_element_type=F32)
+        g = two[:, :128] + two[:, 128:] + one
+        at = pl.multiple_of((yh * nz + z) * 8, 8)
+        for a in range(32):
+            grads[pl.ds(at, 8), a * 128 : (a + 1) * 128] = g[a * 8 : (a + 1) * 8, :]
 
     def step(s, carry):
-        yh = s // (nz // 2)
-        z = (s % (nz // 2)) * 2
-        g = jnp.concatenate([block(z, yh), block(z + 1, yh)], axis=1)
-        hi, lo = split(g)
-        at = pl.multiple_of(s * 16, 16)
-        for a in range(32):
-            g_hi[pl.ds(at, 16), a * 128 : (a + 1) * 128] = hi[a]
-            g_lo[pl.ds(at, 16), a * 128 : (a + 1) * 128] = lo[a]
+        for i in range(UNROLL):
+            block(s * (UNROLL // 2) + i // 2, i % 2, i)
         return carry
 
-    lax.fori_loop(0, nz, step, 0)
+    lax.fori_loop(0, 2 * nz // UNROLL, step, 0)
     dot = functools.partial(lax.dot_general, dimension_numbers=NT, preferred_element_type=F32)
-    p = dot(g_hi[...], f_hi[...]) + dot(g_lo[...], f_hi[...]) + dot(g_hi[...], f_lo[...])
+    wide_rows, width = mine_ref.shape[0], 512
+    p = jnp.zeros((grads.shape[0], 2 * wide_rows), F32)
+    for at in range(0, grads.shape[1], width):
+        columns = slice(at, at + width)
+        g_hi, g_lo = split(grads[:, columns])
+        f = jnp.concatenate([mine_ref[:, columns], other_ref[:, columns]], axis=0)
+        f_hi, f_lo = split(f)
+        two = dot(g_hi, jnp.concatenate([f_hi, f_lo], axis=0))
+        one = dot(g_lo, f_hi)
+        p = p + (two[:, : 2 * wide_rows] + two[:, 2 * wide_rows :] + one)
+    p = jnp.where(core == 0, p, pltpu.roll(p, wide_rows, 1))
     k = exponent(jnp.max(jnp.abs(p), axis=0, keepdims=True))
     rows = p.shape[0]
     out_ref[:rows, :] = coded(p, k)
@@ -164,22 +183,27 @@
             vm,
             pl.BlockSpec(memory_space=pl.ANY),
         ],
-        out_specs=(vm, vm),
-        scratch_shapes=[VMEM((128, 128), F32), pltpu.SemaphoreType.DMA],
+        out_specs=(vm, pl.BlockSpec(memory_space=pl.ANY)),
+        scratch_shapes=[
+            VMEM((128, 128), F32),
+            VMEM((examples, half), BF16),
+            pltpu.SemaphoreType.DMA((CHUNKS,)),
+            pltpu.SemaphoreType.DMA((CHUNKS,)),
+        ],
         compiler_params=grant(60),
     )(query_tokens, token_factors[0], stored)
     tokens = lax.all_gather(tokens, "yh")
     tokens, swapped, fisher = lax.optimization_barrier((tokens, swapped, fisher))
     swapped = swap(swapped, "yh")
     fisher_other = swap(fisher, "c")
-    tokens = lax.all_gather(tokens, "z")
+    tokens = lax.all_gather(tokens, ("z", "c")).reshape(16, 2, 2, 136, 128)
 
     conditioned = pl.pallas_call(
         condition_kernel,
         out_shape=jax.ShapeDtypeStruct((264, 128), I16),
         in_specs=[vm, vm, vm],
         out_specs=vm,
-        scratch_shapes=[VMEM((256, grad), BF16)] * 2 + [VMEM((128, grad), BF16)] * 2,
+        scratch_shapes=[VMEM((256, grad), F32), VMEM((UNROLL, 2, 64, 128), F32)],
         compiler_params=grant(24),
     )(tokens, fisher, fisher_other)
     conditioned = lax.all_gather(conditioned, ("z", "c")).reshape(16, 2, 264, 128)

time: 123 us -> 120 us (0.976)
  Pallas kernels: 13.6 us -> 10.5 us
    all_gather x1, blocking collectives: 38.7 us -> 33.3 us  [body(): lax.all_gather(conditioned, ('z', 'c')).reshape(16, 2, 264, 128)]
    all_gather x1, blocking collectives: 34.9 us -> 40.2 us  [body(): tokens = lax.all_gather(tokens, ('z', 'c')).reshape(16, 2, 2, 136, 128)]
    pallas_call x1, Pallas kernels: 7.71 us -> 4.38 us  [body(): pl.pallas_call(condition_kernel, out_shape=jax.ShapeDtypeStruct((264, 128...]
  transfers between devices with their start and end apart: 2 -> 2, of which waited for: 0 -> 0; matrix products, arithmetic and copies ran while one was open for 0% -> 0% of each run, Pallas kernels for 6% -> 4%
where the time goes in v3:
time: 120 us
  blocking collectives  97.6 us (81%)
  starting transfers between devices  11 us (9%)
  Pallas kernels  10.5 us (9%)
    all_gather x1, blocking collectives, body(): tokens = lax.all_gather(tokens, ('z', 'c')).reshape(16, 2, 2, 136, 128)  40.2 us
    all_gather x1, blocking collectives, body(): lax.all_gather(conditioned, ('z', 'c')).reshape(16, 2, 264, 128)  33.3 us
    all_to_all x1, blocking collectives, body(): lax.all_to_all(partial.reshape(16, 64, examples), ('x', 'yl', 'yh'), 0, 0...  18.2 us
    ppermute x2, starting transfers between devices, swap(): return lax.ppermute(x, axis, [(0, 1), (1, 0)])  11 us
    all_gather x1, blocking collectives, body(): tokens = lax.all_gather(tokens, 'yh')  5.99 us
    pallas_call x1, Pallas kernels, body(): pl.pallas_call(condition_kernel, out_shape=jax.ShapeDtypeStruct((264, 128...  4.38 us
    pallas_call x1, Pallas kernels, body(): pl.pallas_call(encode_kernel, out_shape=(jax.ShapeDtypeStruct((136, 128),...  3.79 us
  transfers between devices with their start and end apart: 2, of which 0 were waited for; matrix products, arithmetic and copies ran while one was open for 0% of the time, Pallas kernels for 4%

profile of v3, /device:TPU:1, one launch (start us, length us, event | category | flops | bytes accessed | tf_op | source)
XLA Modules:
  0.0 119.9 jit_solution(13998543694306337928)
XLA Ops:
  0.0 0.0 copy-start.1
  0.0 3.8 %shard_map.46 = (s16[136,128]{1,0:T(8,128)(2,1)}, bf16[384,2048]{1,0:T(8,128)(2,1)}) custom-call(s32[1,8]{1,0:T(1,128)} %counts_ref.1, f32[128,128]{1,0:T(8,128)} %bitcast.16, bf16[384,4096]{1,0:T(8,128)(2,1)} %bitcast.8), custom_call_target="tpu_custom_call" | custom-call | tf_op jit(solution)/shard_map/pallas_call | solution.py:175
  3.8 6.0 %all-gather = s16[272,128]{1,0:T(8,128)(2,1)S(1)} all-gather(s16[136,128]{1,0:T(8,128)(2,1)} %get-tuple-element.10), channel_id=2, replica_groups=mesh['x'=4,'yl'=2,'yh'=2,'z'=16,'c'=2] {'yh'}, dimensions={0}, use_global_device_ids=true | all-gather | bytes 104448 | tf_op jit(solution)/shard_map/all_gather | solution.py:195
  9.8 0.0 copy-done.1
  9.8 9.1 %collective-permute-start = (f32[64,4096]{1,0:T(8,128)S(1)}, f32[64,4096]{1,0:T(8,128)S(1)}, u32[]{:S(2)}, u32[]{:S(2)}) collective-permute-start(f32[64,4096]{1,0:T(8,128)S(1)} %bitcast.13), channel_id=1, source_target_pairs={{0,1},{1,0},{2,3},{3,2},{4,5},{5,4},{6,7},{7,6},{8,9},{9,8},{10,11... | collective-permute-start | bytes 3145736 | tf_op jit(solution)/shard_map/ppermute | solution.py:165
  18.9 1.9 %collective-permute-start.1 = (bf16[384,2048]{1,0:T(8,128)(2,1)}, bf16[384,2048]{1,0:T(8,128)(2,1)S(1)}, u32[]{:S(2)}, u32[]{:S(2)}) collective-permute-start(bf16[384,2048]{1,0:T(8,128)(2,1)} %get-tuple-element.14), channel_id=1, source_target_pairs={{0,32},{32,0},{1,33},{33,1},{2,34},{34,2},{3,35},{35,3},{4,36},{36... | collective-permute-start | bytes 4718600 | tf_op jit(solution)/shard_map/ppermute | solution.py:165
  20.8 40.2 %all-gather.5 = s16[64,136,128]{2,1,0:T(8,128)(2,1)S(1)} all-gather(s16[2,136,128]{2,1,0:T(8,128)(2,1)S(1)} %bitcast.15), channel_id=3, replica_groups=mesh['x'=4,'yl'=2,'yh'=2,'z'=16,'c'=2] {'z','c'}, dimensions={0}, use_global_device_ids=true | all-gather | bytes 2297856 | tf_op jit(solution)/shard_map/all_gather | solution.py:199
  61.0 0.0 collective-permute-done.other_ref
  61.0 0.0 copy-start
  61.0 4.4 %shard_map.47 = s16[264,128]{1,0:T(8,128)(2,1)S(1)} custom-call(s16[16,2,2,136,128]{4,3,2,1,0:T(8,128)(2,1)S(1)} %bitcast.10, f32[64,4096]{1,0:T(8,128)S(1)} %bitcast.14, f32[64,4096]{1,0:T(8,128)S(1)} %collective-permute-done.other_ref), custom_call_target="tpu_custom_call" | custom-call | tf_op jit(solution)/shard_map/pallas_call | solution.py:201
  65.4 33.3 %all-gather.6 = s16[8448,128]{1,0:T(8,128)(2,1)S(1)} all-gather(s16[264,128]{1,0:T(8,128)(2,1)S(1)} %shard_map.47), channel_id=4, replica_groups=mesh['x'=4,'yl'=2,'yh'=2,'z'=16,'c'=2] {'z','c'}, dimensions={0}, use_global_device_ids=true | all-gather | bytes 2230272 | tf_op jit(solution)/shard_map/all_gather | solution.py:209
  98.7 0.0 collective-permute-done.1.swapped_ref
  98.7 0.0 copy-done
  98.7 2.4 %shard_map.48 = bf16[8,2,64,384]{3,2,1,0:T(8,128)(2,1)S(1)} custom-call(s16[16,2,264,128]{3,2,1,0:T(8,128)(2,1)S(1)} %bitcast.11, bf16[384,4096]{1,0:T(8,128)(2,1)S(1)} %bitcast.9, bf16[384,2048]{1,0:T(8,128)(2,1)S(1)} %collective-permute-done.1.swapped_ref), custom_call_target="tpu_custom_call" | custom-call | tf_op jit(solution)/shard_map/pallas_call | solution.py:211
  101.0 18.2 %all_to_all.5 = bf16[16,64,384]{2,1,0:T(8,128)(2,1)S(1)} all-to-all(bf16[16,64,384]{2,1,0:T(8,128)(2,1)S(1)} %bitcast.12), channel_id=1, replica_groups=mesh['x'=4,'yl'=2,'yh'=2,'z'=16,'c'=2] {'x','yl','yh'}, dimensions={0} | all-to-all | bytes 1572864 | tf_op jit(solution)/shard_map/all_to_all | solution.py:219
  119.2 0.7 convert_reduce_fusion
Async XLA Ops:
  0.0 9.8 %copy-start.1 = (f32[1,64,4096]{2,1,0:T(8,128)S(1)}, f32[1,64,4096]{2,1,0:T(8,128)}, u32[]{:S(2)}) copy-start(f32[1,64,4096]{2,1,0:T(8,128)} %param.6) | copy-start | bytes 3145732
  9.8 51.2 %collective-permute-start = (f32[64,4096]{1,0:T(8,128)S(1)}, f32[64,4096]{1,0:T(8,128)S(1)}, u32[]{:S(2)}, u32[]{:S(2)}) collective-permute-start(f32[64,4096]{1,0:T(8,128)S(1)} %bitcast.13), channel_id=1, source_target_pairs={{0,1},{1,0},{2,3},{3,2},{4,5},{5,4},{6,7},{7,6},{8,9},{9,8},{10,11... | collective-permute-start | bytes 3145736 | tf_op jit(solution)/shard_map/ppermute | solution.py:165
  18.9 79.8 %collective-permute-start.1 = (bf16[384,2048]{1,0:T(8,128)(2,1)}, bf16[384,2048]{1,0:T(8,128)(2,1)S(1)}, u32[]{:S(2)}, u32[]{:S(2)}) collective-permute-start(bf16[384,2048]{1,0:T(8,128)(2,1)} %get-tuple-element.14), channel_id=1, source_target_pairs={{0,32},{32,0},{1,33},{33,1},{2,34},{34,2},{3,35},{35,3},{4,36},{36... | collective-permute-start | bytes 4718600 | tf_op jit(solution)/shard_map/ppermute | solution.py:165
  61.0 37.7 %copy-start = (bf16[1,384,4096]{2,1,0:T(8,128)(2,1)S(1)}, bf16[1,384,4096]{2,1,0:T(8,128)(2,1)}, u32[]{:S(2)}) copy-start(bf16[1,384,4096]{2,1,0:T(8,128)(2,1)} %param.7) | copy-start | bytes 9437188

commit v4 on v3

--- a/solution.py
+++ b/solution.py
@@ -12,7 +12,7 @@
 NT = (((1,), (1,)), ((), ()))
 VMEM = pltpu.VMEM
 UNROLL = 8
-CHUNKS = 6
+ENCODE_MIB = 60
 
 
 def exponent(largest):
@@ -28,21 +28,7 @@
     return hi, (x - hi.astype(F32)).astype(BF16)
 
 
-def encode_kernel(counts_ref, tok_ref, t_ref, out_ref, half_ref, buf, rows, load, store):
-    half = half_ref.shape[1]
-    at = pl.multiple_of((1 - lax.axis_index("yh")) * half, half)
-    chunk = rows.shape[0] // CHUNKS
-    pieces = [pl.ds(i * chunk, chunk) for i in range(CHUNKS)]
-    loads = [
-        pltpu.make_async_copy(t_ref.at[piece, pl.ds(at, half)], rows.at[piece], load.at[i])
-        for i, piece in enumerate(pieces)
-    ]
-    stores = [
-        pltpu.make_async_copy(rows.at[piece], half_ref.at[piece], store.at[i])
-        for i, piece in enumerate(pieces)
-    ]
-    for copy in loads:
-        copy.start()
+def encode_kernel(counts_ref, tok_ref, out_ref, buf):
     buf[...] = tok_ref[...].T
     rank = buf.shape[0] // 2
     ins = buf[:rank, :]
@@ -51,9 +37,6 @@
     k_og = exponent(jnp.max(jnp.abs(ogs), axis=0, keepdims=True))
     t = lax.broadcasted_iota(I32, (1, buf.shape[1]), 1)
     owner = jnp.zeros_like(t)
-    for i in range(CHUNKS // 2):
-        loads[i].wait()
-        stores[i].start()
     end = 0
     for j in range(7):
         end = end + counts_ref[0, j]
@@ -66,20 +49,21 @@
     out_ref[rank : rank + rank // 2, :] = coded(even, k_og)
     out_ref[rank + rank // 2 : 2 * rank, :] = coded(odd, k_og)
     out_ref[2 * rank :, :] = extra.astype(I32).astype(I16)
-    for i in range(CHUNKS // 2, CHUNKS):
-        loads[i].wait()
-        stores[i].start()
-    for copy in stores:
-        copy.wait()
+
+
+def half_kernel(t_ref, tokens_ref, half_ref):
+    half = half_ref.shape[1]
+    at = pl.multiple_of((1 - lax.axis_index("yh")) * half, half)
+    half_ref[...] = t_ref[:, pl.ds(at, half)]
 
 
 def condition_kernel(tok_ref, mine_ref, other_ref, out_ref, grads, wide):
     nz = tok_ref.shape[0]
-    core = lax.axis_index("c")
+    core, home = lax.axis_index("c"), lax.axis_index("yh")
     j = lax.broadcasted_iota(I32, (8, 128), 0).astype(F32)
 
-    def block(z, yh, slot):
-        x = tok_ref[z, core, yh].astype(I32).astype(F32)
+    def block(z, away, slot):
+        x = tok_ref[z, away].astype(I32).astype(F32)
         mask = jnp.where(x[130:131, :] == j, 1.0, 0.0)
         in_hi, in_lo = split(x[0:64, :] * jnp.exp2(x[128:129, :]))
         zero = jnp.zeros((64, 128), BF16)
@@ -110,6 +94,7 @@
         )
         one = lax.dot_general(spread(1), r_hi, NT, preferred_element_type=F32)
         g = two[:, :128] + two[:, 128:] + one
+        yh = 1 - home if away else home
         at = pl.multiple_of((yh * nz + z) * 8, 8)
         for a in range(32):
             grads[pl.ds(at, 8), a * 128 : (a + 1) * 128] = g[a * 8 : (a + 1) * 8, :]
@@ -172,31 +157,25 @@
     half = grad // 2
     vm = pl.BlockSpec(memory_space=VMEM)
 
-    tokens, swapped = pl.pallas_call(
+    tokens = pl.pallas_call(
         encode_kernel,
-        out_shape=(
-            jax.ShapeDtypeStruct((136, 128), I16),
-            jax.ShapeDtypeStruct((examples, half), BF16),
-        ),
-        in_specs=[
-            pl.BlockSpec(memory_space=pltpu.SMEM),
-            vm,
-            pl.BlockSpec(memory_space=pl.ANY),
-        ],
-        out_specs=(vm, pl.BlockSpec(memory_space=pl.ANY)),
-        scratch_shapes=[
-            VMEM((128, 128), F32),
-            VMEM((examples, half), BF16),
-            pltpu.SemaphoreType.DMA((CHUNKS,)),
-            pltpu.SemaphoreType.DMA((CHUNKS,)),
-        ],
-        compiler_params=grant(60),
-    )(query_tokens, token_factors[0], stored)
-    tokens = lax.all_gather(tokens, "yh")
-    tokens, swapped, fisher = lax.optimization_barrier((tokens, swapped, fisher))
+        out_shape=jax.ShapeDtypeStruct((136, 128), I16),
+        in_specs=[pl.BlockSpec(memory_space=pltpu.SMEM), vm],
+        out_specs=vm,
+        scratch_shapes=[VMEM((128, 128), F32)],
+        compiler_params=grant(ENCODE_MIB),
+    )(query_tokens, token_factors[0])
+    away = swap(tokens, "yh")
+    fisher_other = swap(fisher, "c")
+    swapped = pl.pallas_call(
+        half_kernel,
+        out_shape=jax.ShapeDtypeStruct((examples, half), BF16),
+        in_specs=[vm, pl.BlockSpec(memory_space=pl.ANY)],
+        out_specs=vm,
+        compiler_params=grant(8),
+    )(stored, tokens)
     swapped = swap(swapped, "yh")
-    fisher_other = swap(fisher, "c")
-    tokens = lax.all_gather(tokens, ("z", "c")).reshape(16, 2, 2, 136, 128)
+    tokens = lax.all_gather(jnp.concatenate([tokens, away]), "z").reshape(16, 2, 136, 128)
 
     conditioned = pl.pallas_call(
         condition_kernel,

time: 120 us -> 119 us (level)
  blocking collectives: 97.6 us -> 91.3 us
  starting transfers between devices: 11 us -> 15.6 us
  local copies, waits for them, and re-layouts: 0.01 us -> 2.66 us
  Pallas kernels: 10.5 us -> 8.42 us
    all_gather x2 -> x1, blocking collectives: 46.2 us -> 32.2 us  [body(): lax.all_gather(jnp.concatenate([tokens, away]), 'z')]
    all_gather x1, blocking collectives: 33.3 us -> 39 us  [body(): lax.all_gather(conditioned, ('z', 'c')).reshape(16, 2, 264, 128)]
    ppermute x2 -> x3, starting transfers between devices: 11 us -> 15.6 us  [swap(): return lax.ppermute(x, axis, [(0, 1), (1, 0)])]
    unnamed x4 -> x8, local copies, waits for them, and re-layouts: 0.01 us -> 2.66 us
    pallas_call x1 -> x2, Pallas kernels: 3.79 us -> 1.7 us  [the longest x1 1.6 us: body(): pl.pallas_call(encode_kernel, out_shape=jax.ShapeDtypeStruct((136, 128),...]
    all_to_all x1, blocking collectives: 18.2 us -> 20.1 us  [body(): lax.all_to_all(partial.reshape(16, 64, examples), ('x', 'yl', 'yh'), 0, 0...]
  transfers between devices with their start and end apart: 2 -> 3, of which waited for: 0 -> 0; matrix products, arithmetic and copies ran while one was open for 0% -> 0% of each run, Pallas kernels for 4% -> 5%
where the time goes in v4:
time: 119 us
  blocking collectives  91.3 us (77%)
  starting transfers between devices  15.6 us (13%)
  Pallas kernels  8.42 us (7%)
  local copies, waits for them, and re-layouts  2.66 us (2%)
    all_gather x1, blocking collectives, body(): lax.all_gather(conditioned, ('z', 'c')).reshape(16, 2, 264, 128)  39 us
    all_gather x1, blocking collectives, body(): lax.all_gather(jnp.concatenate([tokens, away]), 'z')  32.2 us
    all_to_all x1, blocking collectives, body(): lax.all_to_all(partial.reshape(16, 64, examples), ('x', 'yl', 'yh'), 0, 0...  20.1 us
    ppermute x3, starting transfers between devices, swap(): return lax.ppermute(x, axis, [(0, 1), (1, 0)])  15.6 us
    pallas_call x1, Pallas kernels, body(): pl.pallas_call(condition_kernel, out_shape=jax.ShapeDtypeStruct((264, 128...  4.36 us
    unnamed x8, local copies, waits for them, and re-layouts  2.66 us
  transfers between devices with their start and end apart: 3, of which 0 were waited for; matrix products, arithmetic and copies ran while one was open for 0% of the time, Pallas kernels for 5%

profile of v4, /device:TPU:1, one launch (start us, length us, event | category | flops | bytes accessed | tf_op | source)
XLA Modules:
  0.0 118.8 jit_solution(4570210221091102390)
XLA Ops:
  0.0 8.7 %collective-permute-start.1 = (f32[64,4096]{1,0:T(8,128)}, f32[64,4096]{1,0:T(8,128)S(1)}, u32[]{:S(2)}, u32[]{:S(2)}) collective-permute-start(f32[64,4096]{1,0:T(8,128)} %bitcast.12), channel_id=1, source_target_pairs={{0,1},{1,0},{2,3},{3,2},{4,5},{5,4},{6,7},{7,6},{8,9},{9,8},{10,11... | collective-permute-start | bytes 3145736 | tf_op jit(solution)/shard_map/ppermute | solution.py:150
  8.7 1.6 %shard_map.46.tokens_ref = s16[136,128]{1,0:T(8,128)(2,1)} custom-call(s32[1,8]{1,0:T(1,128)} %counts_ref.1, f32[128,128]{1,0:T(8,128)} %bitcast.14), custom_call_target="tpu_custom_call" | custom-call | tf_op jit(solution)/shard_map/pallas_call | solution.py:160
  10.3 1.9 %collective-permute-start = (s16[136,128]{1,0:T(8,128)(2,1)}, s16[136,128]{1,0:T(8,128)(2,1)S(1)}, u32[]{:S(2)}, u32[]{:S(2)}) collective-permute-start(s16[136,128]{1,0:T(8,128)(2,1)} %shard_map.46.tokens_ref), channel_id=1, source_target_pairs={{0,32},{32,0},{1,33},{33,1},{2,34},{34,2},{3,35},{35,3},{4,36},{36... | collective-permute-start | bytes 104456 | tf_op jit(solution)/shard_map/ppermute | solution.py:150
  12.3 0.0 copy-start
  12.3 1.9 %copy-done = bf16[1,384,4096]{2,1,0:T(8,128)(2,1)S(1)} copy-done((bf16[1,384,4096]{2,1,0:T(8,128)(2,1)S(1)}, bf16[1,384,4096]{2,1,0:T(8,128)(2,1)}, u32[]{:S(2)}) %copy-start) | copy-done | bytes 3145752
  14.2 0.0 copy-start.3
  14.2 0.8 copy-done.3
  14.9 0.1 shard_map.48
  15.0 0.0 copy-start.2
  15.0 5.0 %collective-permute-start.2 = (bf16[384,2048]{1,0:T(8,128)(2,1)S(1)}, bf16[384,2048]{1,0:T(8,128)(2,1)S(1)}, u32[]{:S(2)}, u32[]{:S(2)}) collective-permute-start(bf16[384,2048]{1,0:T(8,128)(2,1)S(1)} %shard_map.48), channel_id=1, source_target_pairs={{0,32},{32,0},{1,33},{33,1},{2,34},{34,2},{3,35},{35,3},{4,36},{36... | collective-permute-start | bytes 4718600 | tf_op jit(solution)/shard_map/ppermute | solution.py:150
  20.0 0.0 collective-permute-done
  20.1 32.2 %all-gather.4 = s16[4352,128]{1,0:T(8,128)(2,1)S(1)} all-gather(s16[272,128]{1,0:T(8,128)(2,1)S(1)} %pad_add_fusion), channel_id=2, replica_groups=mesh['x'=4,'yl'=2,'yh'=2,'z'=16,'c'=2] {'z'}, dimensions={0}, use_global_device_ids=true | all-gather | bytes 1183744 | tf_op jit(solution)/shard_map/all_gather | solution.py:178
  52.3 0.0 collective-permute-done.1.other_ref
  52.3 0.0 copy-done.2
  52.3 0.0 copy-start.1
  52.3 4.4 %shard_map.47 = s16[264,128]{1,0:T(8,128)(2,1)S(1)} custom-call(s16[16,2,136,128]{3,2,1,0:T(8,128)(2,1)S(1)} %bitcast.10, f32[64,4096]{1,0:T(8,128)S(1)} %bitcast.13, f32[64,4096]{1,0:T(8,128)S(1)} %collective-permute-done.1.other_ref), custom_call_target="tpu_custom_call" | custom-call | tf_op jit(solution)/shard_map/pallas_call | solution.py:180
  56.6 39.0 %all-gather.5 = s16[8448,128]{1,0:T(8,128)(2,1)S(1)} all-gather(s16[264,128]{1,0:T(8,128)(2,1)S(1)} %shard_map.47), channel_id=3, replica_groups=mesh['x'=4,'yl'=2,'yh'=2,'z'=16,'c'=2] {'z','c'}, dimensions={0}, use_global_device_ids=true | all-gather | bytes 2230272 | tf_op jit(solution)/shard_map/all_gather | solution.py:188
  95.6 0.0 collective-permute-done.2.swapped_ref
  95.6 0.0 copy-done.1
  95.6 2.4 %shard_map.49 = bf16[8,2,64,384]{3,2,1,0:T(8,128)(2,1)S(1)} custom-call(s16[16,2,264,128]{3,2,1,0:T(8,128)(2,1)S(1)} %bitcast.9, bf16[384,4096]{1,0:T(8,128)(2,1)S(1)} %bitcast.8, bf16[384,2048]{1,0:T(8,128)(2,1)S(1)} %collective-permute-done.2.swapped_ref), custom_call_target="tpu_custom_call" | custom-call | tf_op jit(solution)/shard_map/pallas_call | solution.py:190
  98.0 20.1 %all_to_all.5 = bf16[16,64,384]{2,1,0:T(8,128)(2,1)S(1)} all-to-all(bf16[16,64,384]{2,1,0:T(8,128)(2,1)S(1)} %bitcast.11), channel_id=1, replica_groups=mesh['x'=4,'yl'=2,'yh'=2,'z'=16,'c'=2] {'x','yl','yh'}, dimensions={0} | all-to-all | bytes 1572864 | tf_op jit(solution)/shard_map/all_to_all | solution.py:198
  118.1 0.7 convert_reduce_fusion
  (1 shorter events, 0.0 us)
Async XLA Ops:
  0.0 52.3 %collective-permute-start.1 = (f32[64,4096]{1,0:T(8,128)}, f32[64,4096]{1,0:T(8,128)S(1)}, u32[]{:S(2)}, u32[]{:S(2)}) collective-permute-start(f32[64,4096]{1,0:T(8,128)} %bitcast.12), channel_id=1, source_target_pairs={{0,1},{1,0},{2,3},{3,2},{4,5},{5,4},{6,7},{7,6},{8,9},{9,8},{10,11... | collective-permute-start | bytes 3145736 | tf_op jit(solution)/shard_map/ppermute | solution.py:150
  10.3 9.7 %collective-permute-start = (s16[136,128]{1,0:T(8,128)(2,1)}, s16[136,128]{1,0:T(8,128)(2,1)S(1)}, u32[]{:S(2)}, u32[]{:S(2)}) collective-permute-start(s16[136,128]{1,0:T(8,128)(2,1)} %shard_map.46.tokens_ref), channel_id=1, source_target_pairs={{0,32},{32,0},{1,33},{33,1},{2,34},{34,2},{3,35},{35,3},{4,36},{36... | collective-permute-start | bytes 104456 | tf_op jit(solution)/shard_map/ppermute | solution.py:150
  12.3 1.9 %copy-start = (bf16[1,384,4096]{2,1,0:T(8,128)(2,1)S(1)}, bf16[1,384,4096]{2,1,0:T(8,128)(2,1)}, u32[]{:S(2)}) copy-start(bf16[1,384,4096]{2,1,0:T(8,128)(2,1)} %param.7) | copy-start | bytes 9437188
  14.2 0.8 copy-start.3
  15.0 37.2 %copy-start.2 = (f32[1,64,4096]{2,1,0:T(8,128)S(1)}, f32[1,64,4096]{2,1,0:T(8,128)}, u32[]{:S(2)}) copy-start(f32[1,64,4096]{2,1,0:T(8,128)} %param.6) | copy-start | bytes 3145732
  15.0 80.6 %collective-permute-start.2 = (bf16[384,2048]{1,0:T(8,128)(2,1)S(1)}, bf16[384,2048]{1,0:T(8,128)(2,1)S(1)}, u32[]{:S(2)}, u32[]{:S(2)}) collective-permute-start(bf16[384,2048]{1,0:T(8,128)(2,1)S(1)} %shard_map.48), channel_id=1, source_target_pairs={{0,32},{32,0},{1,33},{33,1},{2,34},{34,2},{3,35},{35,3},{4,36},{36... | collective-permute-start | bytes 4718600 | tf_op jit(solution)/shard_map/ppermute | solution.py:150
  52.3 43.3 %copy-start.1 = (bf16[1,384,4096]{2,1,0:T(8,128)(2,1)S(1)}, bf16[1,384,4096]{2,1,0:T(8,128)(2,1)}, u32[]{:S(2)}) copy-start(bf16[1,384,4096]{2,1,0:T(8,128)(2,1)} %param.7) | copy-start | bytes 9437188

commit v5 on v4

--- a/solution.py
+++ b/solution.py
@@ -13,6 +13,7 @@
 VMEM = pltpu.VMEM
 UNROLL = 8
 ENCODE_MIB = 60
+HALF_MIB = 52
 
 
 def exponent(largest):
@@ -51,19 +52,21 @@
     out_ref[2 * rank :, :] = extra.astype(I32).astype(I16)
 
 
-def half_kernel(t_ref, tokens_ref, half_ref):
+def half_kernel(t_ref, tokens_ref, half_ref, sem):
     half = half_ref.shape[1]
     at = pl.multiple_of((1 - lax.axis_index("yh")) * half, half)
-    half_ref[...] = t_ref[:, pl.ds(at, half)]
+    copy = pltpu.make_async_copy(t_ref.at[:, pl.ds(at, half)], half_ref, sem)
+    copy.start()
+    copy.wait()
 
 
 def condition_kernel(tok_ref, mine_ref, other_ref, out_ref, grads, wide):
     nz = tok_ref.shape[0]
-    core, home = lax.axis_index("c"), lax.axis_index("yh")
+    core = lax.axis_index("c")
     j = lax.broadcasted_iota(I32, (8, 128), 0).astype(F32)
 
-    def block(z, away, slot):
-        x = tok_ref[z, away].astype(I32).astype(F32)
+    def block(z, yh, slot):
+        x = tok_ref[z, yh].astype(I32).astype(F32)
         mask = jnp.where(x[130:131, :] == j, 1.0, 0.0)
         in_hi, in_lo = split(x[0:64, :] * jnp.exp2(x[128:129, :]))
         zero = jnp.zeros((64, 128), BF16)
@@ -94,7 +97,6 @@
         )
         one = lax.dot_general(spread(1), r_hi, NT, preferred_element_type=F32)
         g = two[:, :128] + two[:, 128:] + one
-        yh = 1 - home if away else home
         at = pl.multiple_of((yh * nz + z) * 8, 8)
         for a in range(32):
             grads[pl.ds(at, 8), a * 128 : (a + 1) * 128] = g[a * 8 : (a + 1) * 8, :]
@@ -165,17 +167,18 @@
         scratch_shapes=[VMEM((128, 128), F32)],
         compiler_params=grant(ENCODE_MIB),
     )(query_tokens, token_factors[0])
-    away = swap(tokens, "yh")
+    tokens = lax.all_gather(tokens, "yh")
     fisher_other = swap(fisher, "c")
     swapped = pl.pallas_call(
         half_kernel,
         out_shape=jax.ShapeDtypeStruct((examples, half), BF16),
-        in_specs=[vm, pl.BlockSpec(memory_space=pl.ANY)],
-        out_specs=vm,
-        compiler_params=grant(8),
+        in_specs=[pl.BlockSpec(memory_space=pl.ANY), vm],
+        out_specs=vm,
+        scratch_shapes=[pltpu.SemaphoreType.DMA],
+        compiler_params=grant(HALF_MIB),
     )(stored, tokens)
     swapped = swap(swapped, "yh")
-    tokens = lax.all_gather(jnp.concatenate([tokens, away]), "z").reshape(16, 2, 136, 128)
+    tokens = lax.all_gather(tokens, "z").reshape(16, 2, 136, 128)
 
     conditioned = pl.pallas_call(
         condition_kernel,

time: 119 us -> 120 us (level)
  blocking collectives: 91.3 us -> 97.6 us
  starting transfers between devices: 15.6 us -> 11.3 us
  local copies, waits for them, and re-layouts: 2.66 us -> 0.01 us
  Pallas kernels: 8.42 us -> 9.73 us
    all_gather x1 -> x2, blocking collectives: 32.2 us -> 39.6 us  [the longest x1 34.4 us: body(): tokens = lax.all_gather(tokens, 'z').reshape(16, 2, 136, 128)]
    ppermute x3 -> x2, starting transfers between devices: 15.6 us -> 11.3 us  [swap(): return lax.ppermute(x, axis, [(0, 1), (1, 0)])]
    unnamed x8 -> x4, local copies, waits for them, and re-layouts: 2.66 us -> 0.01 us
    all_to_all x1, blocking collectives: 20.1 us -> 18.1 us  [body(): lax.all_to_all(partial.reshape(16, 64, examples), ('x', 'yl', 'yh'), 0, 0...]
    pallas_call x1, Pallas kernels: 0.1 us -> 1.42 us  [body(): pl.pallas_call(half_kernel, out_shape=jax.ShapeDtypeStruct((examples, hal...]
  transfers between devices with their start and end apart: 3 -> 2, of which waited for: 0 -> 0; matrix products, arithmetic and copies ran while one was open for 0% -> 0% of each run, Pallas kernels for 5% -> 6%
where the time goes in v5:
time: 120 us; the launch traced here: 119 us
  blocking collectives  97.6 us (81%)
  starting transfers between devices  11.3 us (9%)
  Pallas kernels  9.73 us (8%)
    all_gather x1, blocking collectives, body(): lax.all_gather(conditioned, ('z', 'c')).reshape(16, 2, 264, 128)  39.8 us
    all_gather x1, blocking collectives, body(): tokens = lax.all_gather(tokens, 'z').reshape(16, 2, 136, 128)  34.4 us
    all_to_all x1, blocking collectives, body(): lax.all_to_all(partial.reshape(16, 64, examples), ('x', 'yl', 'yh'), 0, 0...  18.1 us
    ppermute x2, starting transfers between devices, swap(): return lax.ppermute(x, axis, [(0, 1), (1, 0)])  11.3 us
    all_gather x1, blocking collectives, body(): tokens = lax.all_gather(tokens, 'yh')  5.15 us
    pallas_call x1, Pallas kernels, body(): pl.pallas_call(condition_kernel, out_shape=jax.ShapeDtypeStruct((264, 128...  4.35 us
  transfers between devices with their start and end apart: 2, of which 0 were waited for; matrix products, arithmetic and copies ran while one was open for 0% of the time, Pallas kernels for 6%

profile of v5, /device:TPU:1, one launch (start us, length us, event | category | flops | bytes accessed | tf_op | source)
XLA Modules:
  0.0 119.4 jit_solution(6114477175240856472)
XLA Ops:
  0.0 8.7 %collective-permute-start = (f32[64,4096]{1,0:T(8,128)}, f32[64,4096]{1,0:T(8,128)S(1)}, u32[]{:S(2)}, u32[]{:S(2)}) collective-permute-start(f32[64,4096]{1,0:T(8,128)} %bitcast.13), channel_id=1, source_target_pairs={{0,1},{1,0},{2,3},{3,2},{4,5},{5,4},{6,7},{7,6},{8,9},{9,8},{10,11... | collective-permute-start | bytes 3145736 | tf_op jit(solution)/shard_map/ppermute | solution.py:152
  8.7 1.6 %shard_map.46 = s16[136,128]{1,0:T(8,128)(2,1)} custom-call(s32[1,8]{1,0:T(1,128)} %counts_ref.1, f32[128,128]{1,0:T(8,128)} %bitcast.17), custom_call_target="tpu_custom_call" | custom-call | tf_op jit(solution)/shard_map/pallas_call | solution.py:162
  10.3 5.2 %all-gather = s16[272,128]{1,0:T(8,128)(2,1)S(1)} all-gather(s16[136,128]{1,0:T(8,128)(2,1)} %shard_map.46), channel_id=2, replica_groups=mesh['x'=4,'yl'=2,'yh'=2,'z'=16,'c'=2] {'yh'}, dimensions={0}, use_global_device_ids=true | all-gather | bytes 104448 | tf_op jit(solution)/shard_map/all_gather | solution.py:170
  15.5 1.4 %shard_map.48 = bf16[384,2048]{1,0:T(8,128)(2,1)S(1)} custom-call(bf16[384,4096]{1,0:T(8,128)(2,1)} %bitcast.8, s16[2,136,128]{2,1,0:T(8,128)(2,1)S(1)} %bitcast.15), custom_call_target="tpu_custom_call" | custom-call | tf_op jit(solution)/shard_map/pallas_call | solution.py:172
  16.9 0.0 copy-start.1
  16.9 2.6 %collective-permute-start.1 = (bf16[384,2048]{1,0:T(8,128)(2,1)S(1)}, bf16[384,2048]{1,0:T(8,128)(2,1)S(1)}, u32[]{:S(2)}, u32[]{:S(2)}) collective-permute-start(bf16[384,2048]{1,0:T(8,128)(2,1)S(1)} %shard_map.48), channel_id=1, source_target_pairs={{0,32},{32,0},{1,33},{33,1},{2,34},{34,2},{3,35},{35,3},{4,36},{36... | collective-permute-start | bytes 4718600 | tf_op jit(solution)/shard_map/ppermute | solution.py:152
  19.5 34.4 %all-gather.5 = s16[32,136,128]{2,1,0:T(8,128)(2,1)S(1)} all-gather(s16[2,136,128]{2,1,0:T(8,128)(2,1)S(1)} %bitcast.16), channel_id=3, replica_groups=mesh['x'=4,'yl'=2,'yh'=2,'z'=16,'c'=2] {'z'}, dimensions={0}, use_global_device_ids=true | all-gather | bytes 1183744 | tf_op jit(solution)/shard_map/all_gather | solution.py:181
  53.9 0.0 collective-permute-done.other_ref
  54.0 0.0 copy-done.1
  54.0 0.0 copy-start
  54.0 4.4 %shard_map.47 = s16[264,128]{1,0:T(8,128)(2,1)S(1)} custom-call(s16[16,2,136,128]{3,2,1,0:T(8,128)(2,1)S(1)} %bitcast.11, f32[64,4096]{1,0:T(8,128)S(1)} %bitcast.14, f32[64,4096]{1,0:T(8,128)S(1)} %collective-permute-done.other_ref), custom_call_target="tpu_custom_call" | custom-call | tf_op jit(solution)/shard_map/pallas_call | solution.py:183
  58.3 39.8 %all-gather.6 = s16[8448,128]{1,0:T(8,128)(2,1)S(1)} all-gather(s16[264,128]{1,0:T(8,128)(2,1)S(1)} %shard_map.47), channel_id=4, replica_groups=mesh['x'=4,'yl'=2,'yh'=2,'z'=16,'c'=2] {'z','c'}, dimensions={0}, use_global_device_ids=true | all-gather | bytes 2230272 | tf_op jit(solution)/shard_map/all_gather | solution.py:191
  98.2 0.0 collective-permute-done.1.swapped_ref
  98.2 0.0 copy-done
  98.2 2.4 %shard_map.49 = bf16[8,2,64,384]{3,2,1,0:T(8,128)(2,1)S(1)} custom-call(s16[16,2,264,128]{3,2,1,0:T(8,128)(2,1)S(1)} %bitcast.10, bf16[384,4096]{1,0:T(8,128)(2,1)S(1)} %bitcast.9, bf16[384,2048]{1,0:T(8,128)(2,1)S(1)} %collective-permute-done.1.swapped_ref), custom_call_target="tpu_custom_call" | custom-call | tf_op jit(solution)/shard_map/pallas_call | solution.py:193
  100.5 18.1 %all_to_all.5 = bf16[16,64,384]{2,1,0:T(8,128)(2,1)S(1)} all-to-all(bf16[16,64,384]{2,1,0:T(8,128)(2,1)S(1)} %bitcast.12), channel_id=1, replica_groups=mesh['x'=4,'yl'=2,'yh'=2,'z'=16,'c'=2] {'x','yl','yh'}, dimensions={0} | all-to-all | bytes 1572864 | tf_op jit(solution)/shard_map/all_to_all | solution.py:201
  118.7 0.7 convert_reduce_fusion
Async XLA Ops:
  0.0 54.0 %collective-permute-start = (f32[64,4096]{1,0:T(8,128)}, f32[64,4096]{1,0:T(8,128)S(1)}, u32[]{:S(2)}, u32[]{:S(2)}) collective-permute-start(f32[64,4096]{1,0:T(8,128)} %bitcast.13), channel_id=1, source_target_pairs={{0,1},{1,0},{2,3},{3,2},{4,5},{5,4},{6,7},{7,6},{8,9},{9,8},{10,11... | collective-permute-start | bytes 3145736 | tf_op jit(solution)/shard_map/ppermute | solution.py:152
  16.9 37.0 %copy-start.1 = (f32[1,64,4096]{2,1,0:T(8,128)S(1)}, f32[1,64,4096]{2,1,0:T(8,128)}, u32[]{:S(2)}) copy-start(f32[1,64,4096]{2,1,0:T(8,128)} %param.6) | copy-start | bytes 3145732
  16.9 81.2 %collective-permute-start.1 = (bf16[384,2048]{1,0:T(8,128)(2,1)S(1)}, bf16[384,2048]{1,0:T(8,128)(2,1)S(1)}, u32[]{:S(2)}, u32[]{:S(2)}) collective-permute-start(bf16[384,2048]{1,0:T(8,128)(2,1)S(1)} %shard_map.48), channel_id=1, source_target_pairs={{0,32},{32,0},{1,33},{33,1},{2,34},{34,2},{3,35},{35,3},{4,36},{36... | collective-permute-start | bytes 4718600 | tf_op jit(solution)/shard_map/ppermute | solution.py:152
  54.0 44.2 %copy-start = (bf16[1,384,4096]{2,1,0:T(8,128)(2,1)S(1)}, bf16[1,384,4096]{2,1,0:T(8,128)(2,1)}, u32[]{:S(2)}) copy-start(bf16[1,384,4096]{2,1,0:T(8,128)(2,1)} %param.7) | copy-start | bytes 9437188

commit v6 on v4

--- a/solution.py
+++ b/solution.py
@@ -51,19 +51,12 @@
     out_ref[2 * rank :, :] = extra.astype(I32).astype(I16)
 
 
-def half_kernel(t_ref, tokens_ref, half_ref):
-    half = half_ref.shape[1]
-    at = pl.multiple_of((1 - lax.axis_index("yh")) * half, half)
-    half_ref[...] = t_ref[:, pl.ds(at, half)]
-
-
 def condition_kernel(tok_ref, mine_ref, other_ref, out_ref, grads, wide):
-    nz = tok_ref.shape[0]
-    core, home = lax.axis_index("c"), lax.axis_index("yh")
+    nz, nc = tok_ref.shape[:2]
     j = lax.broadcasted_iota(I32, (8, 128), 0).astype(F32)
 
-    def block(z, away, slot):
-        x = tok_ref[z, away].astype(I32).astype(F32)
+    def block(z, c, slot):
+        x = tok_ref[z, c].astype(I32).astype(F32)
         mask = jnp.where(x[130:131, :] == j, 1.0, 0.0)
         in_hi, in_lo = split(x[0:64, :] * jnp.exp2(x[128:129, :]))
         zero = jnp.zeros((64, 128), BF16)
@@ -94,8 +87,7 @@
         )
         one = lax.dot_general(spread(1), r_hi, NT, preferred_element_type=F32)
         g = two[:, :128] + two[:, 128:] + one
-        yh = 1 - home if away else home
-        at = pl.multiple_of((yh * nz + z) * 8, 8)
+        at = pl.multiple_of((z * nc + c) * 8, 8)
         for a in range(32):
             grads[pl.ds(at, 8), a * 128 : (a + 1) * 128] = g[a * 8 : (a + 1) * 8, :]
 
@@ -104,7 +96,7 @@
             block(s * (UNROLL // 2) + i // 2, i % 2, i)
         return carry
 
-    lax.fori_loop(0, 2 * nz // UNROLL, step, 0)
+    lax.fori_loop(0, nc * nz // UNROLL, step, 0)
     dot = functools.partial(lax.dot_general, dimension_numbers=NT, preferred_element_type=F32)
     wide_rows, width = mine_ref.shape[0], 512
     p = jnp.zeros((grads.shape[0], 2 * wide_rows), F32)
@@ -116,30 +108,29 @@
         two = dot(g_hi, jnp.concatenate([f_hi, f_lo], axis=0))
         one = dot(g_lo, f_hi)
         p = p + (two[:, : 2 * wide_rows] + two[:, 2 * wide_rows :] + one)
-    p = jnp.where(core == 0, p, pltpu.roll(p, wide_rows, 1))
+    p = jnp.where(lax.axis_index("c") == lax.axis_index("yh"), p, pltpu.roll(p, wide_rows, 1))
     k = exponent(jnp.max(jnp.abs(p), axis=0, keepdims=True))
     rows = p.shape[0]
     out_ref[:rows, :] = coded(p, k)
     out_ref[rows:, :] = jnp.broadcast_to(k, (8, 128)).astype(I32).astype(I16)
 
 
-def score_kernel(p_ref, t_ref, swapped_ref, out_ref, p_all):
-    nz = p_ref.shape[0]
-    half = swapped_ref.shape[1]
-    yh = lax.axis_index("yh")
+def score_kernel(p_ref, t_ref, out_ref, p_all):
+    nz, _, ny, rows, lanes = p_ref.shape
+    rows = rows - 8
+    first = lax.broadcasted_iota(I32, (rows, lanes), 1) < lanes // 2
     for z in range(nz):
-        parts = []
-        for c in range(2):
-            v = p_ref[z, c].astype(I32).astype(F32)
-            parts.append((v[:256, :] * jnp.exp2(v[256:257, :])).reshape(32, 8, 128))
-        p_all[:, z * 128 : (z + 1) * 128] = (
-            jnp.concatenate(parts, axis=1).reshape(512, 128).astype(BF16)
-        )
-    own = t_ref[:, pl.ds(pl.multiple_of(yh * half, half), half)]
-    for t, at in ((own, yh), (swapped_ref[...], 1 - yh)):
-        s = lax.dot_general(p_all[...], t, NT, preferred_element_type=F32).astype(BF16)
-        for m in range(8):
-            out_ref[m, at] = s[m * 64 : (m + 1) * 64, :]
+        for yh in range(ny):
+            v = [p_ref[z, c, yh].astype(I32).astype(F32) for c in range(2)]
+            v = [u[:rows, :] * jnp.exp2(u[rows : rows + 1, :]) for u in v]
+            low = jnp.where(first, v[0], v[1])
+            high = pltpu.roll(jnp.where(first, v[1], v[0]), lanes // 2, 1)
+            for half, tile in ((0, low), (1, high)):
+                at = (half * nz + z) * lanes
+                p_all[yh * rows : (yh + 1) * rows, at : at + lanes] = tile.astype(BF16)
+    s = lax.dot_general(p_all[...], t_ref[...], NT, preferred_element_type=F32).astype(BF16)
+    for m in range(8):
+        out_ref[m] = s[m * 64 : (m + 1) * 64, :]
 
 
 def grant(mib):
@@ -154,7 +145,6 @@
     fisher = fisher_inverse[0]
     stored = train_grads[0]
     examples, grad = stored.shape
-    half = grad // 2
     vm = pl.BlockSpec(memory_space=VMEM)
 
     tokens = pl.pallas_call(
@@ -165,17 +155,8 @@
         scratch_shapes=[VMEM((128, 128), F32)],
         compiler_params=grant(ENCODE_MIB),
     )(query_tokens, token_factors[0])
-    away = swap(tokens, "yh")
-    fisher_other = swap(fisher, "c")
-    swapped = pl.pallas_call(
-        half_kernel,
-        out_shape=jax.ShapeDtypeStruct((examples, half), BF16),
-        in_specs=[vm, pl.BlockSpec(memory_space=pl.ANY)],
-        out_specs=vm,
-        compiler_params=grant(8),
-    )(stored, tokens)
-    swapped = swap(swapped, "yh")
-    tokens = lax.all_gather(jnp.concatenate([tokens, away]), "z").reshape(16, 2, 136, 128)
+    fisher_other = swap(fisher, "yh")
+    tokens = lax.all_gather(tokens, ("z", "c")).reshape(16, 2, 136, 128)
 
     conditioned = pl.pallas_call(
         condition_kernel,
@@ -185,19 +166,18 @@
         scratch_shapes=[VMEM((256, grad), F32), VMEM((UNROLL, 2, 64, 128), F32)],
         compiler_params=grant(24),
     )(tokens, fisher, fisher_other)
-    conditioned = lax.all_gather(conditioned, ("z", "c")).reshape(16, 2, 264, 128)
+    conditioned = lax.all_gather(conditioned, "yh")
+    conditioned = lax.all_gather(conditioned, ("z", "c")).reshape(16, 2, 2, 264, 128)
 
     partial = pl.pallas_call(
         score_kernel,
-        out_shape=jax.ShapeDtypeStruct((8, 2, 64, examples), BF16),
-        in_specs=[vm, vm, vm],
+        out_shape=jax.ShapeDtypeStruct((8, 64, examples), BF16),
+        in_specs=[vm, vm],
         out_specs=vm,
-        scratch_shapes=[VMEM((512, half), BF16)],
+        scratch_shapes=[VMEM((512, grad), BF16)],
         compiler_params=grant(24),
-    )(conditioned, stored, swapped)
-    partial = lax.all_to_all(
-        partial.reshape(16, 64, examples), ("x", "yl", "yh"), 0, 0, tiled=True
-    )
+    )(conditioned, stored)
+    partial = lax.all_to_all(partial, ("x", "yl"), 0, 0, tiled=True)
     return jnp.sum(partial.astype(F32), axis=0).T
 
 

time: 119 us -> 119 us (level)
  blocking collectives: 91.3 us -> 102 us
  starting transfers between devices: 15.6 us -> 5.63 us
  local copies, waits for them, and re-layouts: 2.66 us -> 1.23 us
    all_gather x2 -> x3, blocking collectives: 71.2 us -> 90.1 us  [the longest x1 43.9 us: body(): lax.all_gather(conditioned, ('z', 'c')).reshape(16, 2, 2, 264, 128)]
    ppermute x3 -> x1, starting transfers between devices: 15.6 us -> 5.63 us  [swap(): return lax.ppermute(x, axis, [(0, 1), (1, 0)])]
    all_to_all x1, blocking collectives: 20.1 us -> 11.8 us  [body(): partial = lax.all_to_all(partial, ('x', 'yl'), 0, 0, tiled=True)]
    unnamed x8 -> x4, local copies, waits for them, and re-layouts: 2.66 us -> 1.23 us
    pallas_call x2 -> x1, Pallas kernels: 2.46 us -> 2.97 us  [body(): pl.pallas_call(score_kernel, out_shape=jax.ShapeDtypeStruct((8, 64, examp...]
  transfers between devices with their start and end apart: 3 -> 1, of which waited for: 0 -> 0; matrix products, arithmetic and copies ran while one was open for 0% -> 0% of each run, Pallas kernels for 5% -> 1%
where the time goes in v6:
time: 119 us; the launch traced here: 118 us
  blocking collectives  102 us (86%)
  Pallas kernels  8.93 us (8%)
  starting transfers between devices  5.63 us (5%)
  local copies, waits for them, and re-layouts  1.23 us (1%)
    all_gather x1, blocking collectives, body(): lax.all_gather(conditioned, ('z', 'c')).reshape(16, 2, 2, 264, 128)  43.9 us
    all_gather x1, blocking collectives, body(): tokens = lax.all_gather(tokens, ('z', 'c')).reshape(16, 2, 136, 128)  40.3 us
    all_to_all x1, blocking collectives, body(): partial = lax.all_to_all(partial, ('x', 'yl'), 0, 0, tiled=True)  11.8 us
    all_gather x1, blocking collectives, body(): conditioned = lax.all_gather(conditioned, 'yh')  5.84 us
    ppermute x1, starting transfers between devices, swap(): return lax.ppermute(x, axis, [(0, 1), (1, 0)])  5.63 us
    pallas_call x1, Pallas kernels, body(): pl.pallas_call(condition_kernel, out_shape=jax.ShapeDtypeStruct((264, 128...  4.36 us
    pallas_call x1, Pallas kernels, body(): pl.pallas_call(score_kernel, out_shape=jax.ShapeDtypeStruct((8, 64, examp...  2.97 us
  transfers between devices with their start and end apart: 1, of which 0 were waited for; matrix products, arithmetic and copies ran while one was open for 0% of the time, Pallas kernels for 1%

profile of v6, /device:TPU:1, one launch (start us, length us, event | category | flops | bytes accessed | tf_op | source)
XLA Modules:
  0.0 118.3 jit_solution(1950587653678315493)
XLA Ops:
  0.0 5.6 %collective-permute-start = (f32[64,4096]{1,0:T(8,128)}, f32[64,4096]{1,0:T(8,128)S(1)}, u32[]{:S(2)}, u32[]{:S(2)}) collective-permute-start(f32[64,4096]{1,0:T(8,128)} %bitcast.10), channel_id=1, source_target_pairs={{0,32},{32,0},{1,33},{33,1},{2,34},{34,2},{3,35},{35,3},{4,36},{36... | collective-permute-start | bytes 3145736 | tf_op jit(solution)/shard_map/ppermute | solution.py:141
  5.6 1.6 %shard_map.46 = s16[136,128]{1,0:T(8,128)(2,1)} custom-call(s32[1,8]{1,0:T(1,128)} %counts_ref.1, f32[128,128]{1,0:T(8,128)} %bitcast.13), custom_call_target="tpu_custom_call" | custom-call | tf_op jit(solution)/shard_map/pallas_call | solution.py:150
  7.2 40.3 %all-gather.5 = s16[4352,128]{1,0:T(8,128)(2,1)S(1)} all-gather(s16[136,128]{1,0:T(8,128)(2,1)} %shard_map.46), channel_id=2, replica_groups=mesh['x'=4,'yl'=2,'yh'=2,'z'=16,'c'=2] {'z','c'}, dimensions={0}, use_global_device_ids=true | all-gather | bytes 1148928 | tf_op jit(solution)/shard_map/all_gather | solution.py:159
  47.5 0.0 collective-permute-done.other_ref
  47.5 0.0 copy-start.1
  47.5 1.2 %copy-done.1 = f32[1,64,4096]{2,1,0:T(8,128)S(1)} copy-done((f32[1,64,4096]{2,1,0:T(8,128)S(1)}, f32[1,64,4096]{2,1,0:T(8,128)}, u32[]{:S(2)}) %copy-start.1) | copy-done | bytes 1048600
  48.7 4.4 %shard_map.47 = s16[264,128]{1,0:T(8,128)(2,1)S(1)} custom-call(s16[16,2,136,128]{3,2,1,0:T(8,128)(2,1)S(1)} %bitcast.8, f32[64,4096]{1,0:T(8,128)S(1)} %bitcast.11, f32[64,4096]{1,0:T(8,128)S(1)} %collective-permute-done.other_ref), custom_call_target="tpu_custom_call" | custom-call | tf_op jit(solution)/shard_map/pallas_call | solution.py:161
  53.1 0.0 copy-start
  53.1 5.8 %all-gather.1 = s16[528,128]{1,0:T(8,128)(2,1)S(1)} all-gather(s16[264,128]{1,0:T(8,128)(2,1)S(1)} %shard_map.47), channel_id=3, replica_groups=mesh['x'=4,'yl'=2,'yh'=2,'z'=16,'c'=2] {'yh'}, dimensions={0}, use_global_device_ids=true | all-gather | bytes 202752 | tf_op jit(solution)/shard_map/all_gather | solution.py:169
  59.0 43.9 %all-gather.6 = s16[64,264,128]{2,1,0:T(8,128)(2,1)S(1)} all-gather(s16[2,264,128]{2,1,0:T(8,128)(2,1)S(1)} %bitcast.12), channel_id=4, replica_groups=mesh['x'=4,'yl'=2,'yh'=2,'z'=16,'c'=2] {'z','c'}, dimensions={0}, use_global_device_ids=true | all-gather | bytes 4460544 | tf_op jit(solution)/shard_map/all_gather | solution.py:170
  102.9 0.0 copy-done
  102.9 3.0 %shard_map.48 = bf16[8,64,384]{2,1,0:T(8,128)(2,1)S(1)} custom-call(s16[16,2,2,264,128]{4,3,2,1,0:T(8,128)(2,1)S(1)} %bitcast.7, bf16[384,4096]{1,0:T(8,128)(2,1)S(1)} %bitcast.9), custom_call_target="tpu_custom_call" | custom-call | tf_op jit(solution)/shard_map/pallas_call | solution.py:172
  105.9 11.8 %all_to_all.5 = bf16[8,64,384]{2,1,0:T(8,128)(2,1)S(1)} all-to-all(bf16[8,64,384]{2,1,0:T(8,128)(2,1)S(1)} %shard_map.48), channel_id=1, replica_groups=mesh['x'=4,'yl'=2,'yh'=2,'z'=16,'c'=2] {'x','yl'}, dimensions={0} | all-to-all | bytes 786432 | tf_op jit(solution)/shard_map/all_to_all | solution.py:180
  117.7 0.7 convert_reduce_fusion
Async XLA Ops:
  0.0 47.5 %collective-permute-start = (f32[64,4096]{1,0:T(8,128)}, f32[64,4096]{1,0:T(8,128)S(1)}, u32[]{:S(2)}, u32[]{:S(2)}) collective-permute-start(f32[64,4096]{1,0:T(8,128)} %bitcast.10), channel_id=1, source_target_pairs={{0,32},{32,0},{1,33},{33,1},{2,34},{34,2},{3,35},{35,3},{4,36},{36... | collective-permute-start | bytes 3145736 | tf_op jit(solution)/shard_map/ppermute | solution.py:141
  47.5 1.2 %copy-start.1 = (f32[1,64,4096]{2,1,0:T(8,128)S(1)}, f32[1,64,4096]{2,1,0:T(8,128)}, u32[]{:S(2)}) copy-start(f32[1,64,4096]{2,1,0:T(8,128)} %param.6) | copy-start | bytes 3145732
  53.1 49.8 %copy-start = (bf16[1,384,4096]{2,1,0:T(8,128)(2,1)S(1)}, bf16[1,384,4096]{2,1,0:T(8,128)(2,1)}, u32[]{:S(2)}) copy-start(bf16[1,384,4096]{2,1,0:T(8,128)(2,1)} %param.7) | copy-start | bytes 9437188

commit v7 on v6

--- a/solution.py
+++ b/solution.py
@@ -12,7 +12,7 @@
 NT = (((1,), (1,)), ((), ()))
 VMEM = pltpu.VMEM
 UNROLL = 8
-ENCODE_MIB = 60
+ENCODE_MIB = 8
 
 
 def exponent(largest):
@@ -51,7 +51,9 @@
     out_ref[2 * rank :, :] = extra.astype(I32).astype(I16)
 
 
-def condition_kernel(tok_ref, mine_ref, other_ref, out_ref, grads, wide):
+def condition_kernel(tok_ref, rows_ref, other_ref, out_ref, grads, wide, mine_ref, sem):
+    load = pltpu.make_async_copy(rows_ref, mine_ref, sem)
+    load.start()
     nz, nc = tok_ref.shape[:2]
     j = lax.broadcasted_iota(I32, (8, 128), 0).astype(F32)
 
@@ -98,6 +100,7 @@
 
     lax.fori_loop(0, nc * nz // UNROLL, step, 0)
     dot = functools.partial(lax.dot_general, dimension_numbers=NT, preferred_element_type=F32)
+    load.wait()
     wide_rows, width = mine_ref.shape[0], 512
     p = jnp.zeros((grads.shape[0], 2 * wide_rows), F32)
     for at in range(0, grads.shape[1], width):
@@ -137,6 +140,10 @@
     return pltpu.CompilerParams(vmem_limit_bytes=mib << 20)
 
 
+def in_hbm(x):
+    return pltpu.with_memory_space_constraint(x, pltpu.HBM)
+
+
 def swap(x, axis):
     return lax.ppermute(x, axis, [(0, 1), (1, 0)])
 
@@ -149,23 +156,28 @@
 
     tokens = pl.pallas_call(
         encode_kernel,
-        out_shape=jax.ShapeDtypeStruct((136, 128), I16),
+        out_shape=pltpu.VMEM((136, 128), I16),
         in_specs=[pl.BlockSpec(memory_space=pltpu.SMEM), vm],
         out_specs=vm,
         scratch_shapes=[VMEM((128, 128), F32)],
         compiler_params=grant(ENCODE_MIB),
-    )(query_tokens, token_factors[0])
+    )(in_hbm(query_tokens), in_hbm(token_factors[0]))
     fisher_other = swap(fisher, "yh")
     tokens = lax.all_gather(tokens, ("z", "c")).reshape(16, 2, 136, 128)
 
     conditioned = pl.pallas_call(
         condition_kernel,
         out_shape=jax.ShapeDtypeStruct((264, 128), I16),
-        in_specs=[vm, vm, vm],
+        in_specs=[vm, pl.BlockSpec(memory_space=pl.ANY), vm],
         out_specs=vm,
-        scratch_shapes=[VMEM((256, grad), F32), VMEM((UNROLL, 2, 64, 128), F32)],
+        scratch_shapes=[
+            VMEM((256, grad), F32),
+            VMEM((UNROLL, 2, 64, 128), F32),
+            VMEM(fisher.shape, F32),
+            pltpu.SemaphoreType.DMA,
+        ],
         compiler_params=grant(24),
-    )(tokens, fisher, fisher_other)
+    )(tokens, in_hbm(fisher), fisher_other)
     conditioned = lax.all_gather(conditioned, "yh")
     conditioned = lax.all_gather(conditioned, ("z", "c")).reshape(16, 2, 2, 264, 128)
 

time: 119 us -> 117 us (0.983)
  local copies, waits for them, and re-layouts: 1.23 us -> 0.01 us
    unnamed x4 -> x2, local copies, waits for them, and re-layouts: 1.23 us -> 0.01 us
where the time goes in v7:
time: 117 us; the launch traced here: 116 us
  blocking collectives  102 us (87%)
  Pallas kernels  8.35 us (7%)
  starting transfers between devices  5.63 us (5%)
    all_gather x1, blocking collectives, body(): lax.all_gather(conditioned, ('z', 'c')).reshape(16, 2, 2, 264, 128)  44 us
    all_gather x1, blocking collectives, body(): tokens = lax.all_gather(tokens, ('z', 'c')).reshape(16, 2, 136, 128)  40.1 us
    all_to_all x1, blocking collectives, body(): partial = lax.all_to_all(partial, ('x', 'yl'), 0, 0, tiled=True)  11.8 us
    all_gather x1, blocking collectives, body(): conditioned = lax.all_gather(conditioned, 'yh')  5.83 us
    ppermute x1, starting transfers between devices, swap(): return lax.ppermute(x, axis, [(0, 1), (1, 0)])  5.63 us
    pallas_call x1, Pallas kernels, body(): pl.pallas_call(condition_kernel, out_shape=jax.ShapeDtypeStruct((264, 128...  4.41 us
    pallas_call x1, Pallas kernels, body(): pl.pallas_call(score_kernel, out_shape=jax.ShapeDtypeStruct((8, 64, examp...  2.97 us
  transfers between devices with their start and end apart: 1, of which 0 were waited for; matrix products, arithmetic and copies ran while one was open for 0% of the time, Pallas kernels for 1%

profile of v7, /device:TPU:1, one launch (start us, length us, event | category | flops | bytes accessed | tf_op | source)
XLA Modules:
  0.0 116.3 jit_solution(17871794018430585960)
XLA Ops:
  0.0 5.6 %collective-permute-start = (f32[64,4096]{1,0:T(8,128)}, f32[64,4096]{1,0:T(8,128)S(1)}, u32[]{:S(2)}, u32[]{:S(2)}) collective-permute-start(f32[64,4096]{1,0:T(8,128)} %bitcast.10), channel_id=1, source_target_pairs={{0,32},{32,0},{1,33},{33,1},{2,34},{34,2},{3,35},{35,3},{4,36},{36... | collective-permute-start | bytes 3145736 | tf_op jit(solution)/shard_map/ppermute | solution.py:148
  5.6 1.0 shard_map.46
  6.6 40.1 %all-gather.5 = s16[4352,128]{1,0:T(8,128)(2,1)S(1)} all-gather(s16[136,128]{1,0:T(8,128)(2,1)S(1)} %shard_map.46), channel_id=2, replica_groups=mesh['x'=4,'yl'=2,'yh'=2,'z'=16,'c'=2] {'z','c'}, dimensions={0}, use_global_device_ids=true | all-gather | bytes 1148928 | tf_op jit(solution)/shard_map/all_gather | solution.py:166
  46.7 0.0 collective-permute-done.other_ref
  46.7 4.4 %shard_map.47 = s16[264,128]{1,0:T(8,128)(2,1)S(1)} custom-call(s16[16,2,136,128]{3,2,1,0:T(8,128)(2,1)S(1)} %bitcast.8, f32[64,4096]{1,0:T(8,128)} %bitcast.11, f32[64,4096]{1,0:T(8,128)S(1)} %collective-permute-done.other_ref), custom_call_target="tpu_custom_call" | custom-call | tf_op jit(solution)/shard_map/pallas_call | solution.py:168
  51.1 0.0 copy-start
  51.1 5.8 %all-gather.1 = s16[528,128]{1,0:T(8,128)(2,1)S(1)} all-gather(s16[264,128]{1,0:T(8,128)(2,1)S(1)} %shard_map.47), channel_id=3, replica_groups=mesh['x'=4,'yl'=2,'yh'=2,'z'=16,'c'=2] {'yh'}, dimensions={0}, use_global_device_ids=true | all-gather | bytes 202752 | tf_op jit(solution)/shard_map/all_gather | solution.py:181
  56.9 44.0 %all-gather.6 = s16[64,264,128]{2,1,0:T(8,128)(2,1)S(1)} all-gather(s16[2,264,128]{2,1,0:T(8,128)(2,1)S(1)} %bitcast.12), channel_id=4, replica_groups=mesh['x'=4,'yl'=2,'yh'=2,'z'=16,'c'=2] {'z','c'}, dimensions={0}, use_global_device_ids=true | all-gather | bytes 4460544 | tf_op jit(solution)/shard_map/all_gather | solution.py:182
  100.9 0.0 copy-done
  100.9 3.0 %shard_map.48 = bf16[8,64,384]{2,1,0:T(8,128)(2,1)S(1)} custom-call(s16[16,2,2,264,128]{4,3,2,1,0:T(8,128)(2,1)S(1)} %bitcast.7, bf16[384,4096]{1,0:T(8,128)(2,1)S(1)} %bitcast.9), custom_call_target="tpu_custom_call" | custom-call | tf_op jit(solution)/shard_map/pallas_call | solution.py:184
  103.9 11.8 %all_to_all.5 = bf16[8,64,384]{2,1,0:T(8,128)(2,1)S(1)} all-to-all(bf16[8,64,384]{2,1,0:T(8,128)(2,1)S(1)} %shard_map.48), channel_id=1, replica_groups=mesh['x'=4,'yl'=2,'yh'=2,'z'=16,'c'=2] {'x','yl'}, dimensions={0} | all-to-all | bytes 786432 | tf_op jit(solution)/shard_map/all_to_all | solution.py:192
  115.7 0.7 convert_reduce_fusion
Async XLA Ops:
  0.0 46.7 %collective-permute-start = (f32[64,4096]{1,0:T(8,128)}, f32[64,4096]{1,0:T(8,128)S(1)}, u32[]{:S(2)}, u32[]{:S(2)}) collective-permute-start(f32[64,4096]{1,0:T(8,128)} %bitcast.10), channel_id=1, source_target_pairs={{0,32},{32,0},{1,33},{33,1},{2,34},{34,2},{3,35},{35,3},{4,36},{36... | collective-permute-start | bytes 3145736 | tf_op jit(solution)/shard_map/ppermute | solution.py:148
  51.1 49.8 %copy-start = (bf16[1,384,4096]{2,1,0:T(8,128)(2,1)S(1)}, bf16[1,384,4096]{2,1,0:T(8,128)(2,1)}, u32[]{:S(2)}) copy-start(bf16[1,384,4096]{2,1,0:T(8,128)(2,1)} %param.7) | copy-start | bytes 9437188

commit v8 on v7

--- a/solution.py
+++ b/solution.py
@@ -29,13 +29,14 @@
 
 
 def encode_kernel(counts_ref, tok_ref, out_ref, buf):
-    buf[...] = tok_ref[...].T
-    rank = buf.shape[0] // 2
-    ins = buf[:rank, :]
-    ogs = buf[rank:, :]
+    x = tok_ref[...].T
+    rank = x.shape[0] // 2
+    buf[: 2 * rank, :] = x
+    ins = x[:rank, :]
+    ogs = x[rank:, :]
     k_in = exponent(jnp.max(jnp.abs(ins), axis=0, keepdims=True))
     k_og = exponent(jnp.max(jnp.abs(ogs), axis=0, keepdims=True))
-    t = lax.broadcasted_iota(I32, (1, buf.shape[1]), 1)
+    t = lax.broadcasted_iota(I32, (1, x.shape[1]), 1)
     owner = jnp.zeros_like(t)
     end = 0
     for j in range(7):
@@ -43,7 +44,7 @@
         owner = owner + (t >= end).astype(I32)
     even = buf[pl.ds(rank, rank // 2, stride=2), :]
     odd = buf[pl.ds(rank + 1, rank // 2, stride=2), :]
-    row = lax.broadcasted_iota(I32, (8, buf.shape[1]), 0)
+    row = lax.broadcasted_iota(I32, (8, x.shape[1]), 0)
     extra = jnp.where(row == 0, k_in, jnp.where(row == 1, k_og, owner.astype(F32)))
     out_ref[:rank, :] = coded(ins, k_in)
     out_ref[rank : rank + rank // 2, :] = coded(even, k_og)
@@ -71,8 +72,8 @@
         r_hi, r_lo = diagonal(in_hi), diagonal(in_lo)
         w = x[64:128, :] * jnp.exp2(x[129:130, :])
         hi = w.astype(BF16).astype(F32)
-        wide[slot, 0] = hi
-        wide[slot, 1] = w - hi
+        wide[slot, 0, 0:64, :] = hi
+        wide[slot, 1, 0:64, :] = w - hi
 
         def spread(part):
             halves = []
@@ -159,7 +160,7 @@
         out_shape=pltpu.VMEM((136, 128), I16),
         in_specs=[pl.BlockSpec(memory_space=pltpu.SMEM), vm],
         out_specs=vm,
-        scratch_shapes=[VMEM((128, 128), F32)],
+        scratch_shapes=[VMEM((136, 128), F32)],
         compiler_params=grant(ENCODE_MIB),
     )(in_hbm(query_tokens), in_hbm(token_factors[0]))
     fisher_other = swap(fisher, "yh")
@@ -172,7 +173,7 @@
         out_specs=vm,
         scratch_shapes=[
             VMEM((256, grad), F32),
-            VMEM((UNROLL, 2, 64, 128), F32),
+            VMEM((UNROLL, 2, 72, 128), F32),
             VMEM(fisher.shape, F32),
             pltpu.SemaphoreType.DMA,
         ],

time: 117 us -> 117 us (level)
  no operation moved by 1% of the time
where the time goes in v8:
time: 117 us; the launch traced here: 116 us
  blocking collectives  102 us (87%)
  Pallas kernels  8.35 us (7%)
  starting transfers between devices  5.63 us (5%)
    all_gather x1, blocking collectives, body(): lax.all_gather(conditioned, ('z', 'c')).reshape(16, 2, 2, 264, 128)  44 us
    all_gather x1, blocking collectives, body(): tokens = lax.all_gather(tokens, ('z', 'c')).reshape(16, 2, 136, 128)  40.1 us
    all_to_all x1, blocking collectives, body(): partial = lax.all_to_all(partial, ('x', 'yl'), 0, 0, tiled=True)  11.8 us
    all_gather x1, blocking collectives, body(): conditioned = lax.all_gather(conditioned, 'yh')  5.83 us
    ppermute x1, starting transfers between devices, swap(): return lax.ppermute(x, axis, [(0, 1), (1, 0)])  5.63 us
    pallas_call x1, Pallas kernels, body(): pl.pallas_call(condition_kernel, out_shape=jax.ShapeDtypeStruct((264, 128...  4.41 us
    pallas_call x1, Pallas kernels, body(): pl.pallas_call(score_kernel, out_shape=jax.ShapeDtypeStruct((8, 64, examp...  2.97 us
  transfers between devices with their start and end apart: 1, of which 0 were waited for; matrix products, arithmetic and copies ran while one was open for 0% of the time, Pallas kernels for 1%

profile of v8, /device:TPU:1, one launch (start us, length us, event | category | flops | bytes accessed | tf_op | source)
XLA Modules:
  0.0 116.3 jit_solution(10646113281197073894)
XLA Ops:
  0.0 5.6 %collective-permute-start = (f32[64,4096]{1,0:T(8,128)}, f32[64,4096]{1,0:T(8,128)S(1)}, u32[]{:S(2)}, u32[]{:S(2)}) collective-permute-start(f32[64,4096]{1,0:T(8,128)} %bitcast.10), channel_id=1, source_target_pairs={{0,32},{32,0},{1,33},{33,1},{2,34},{34,2},{3,35},{35,3},{4,36},{36... | collective-permute-start | bytes 3145736 | tf_op jit(solution)/shard_map/ppermute | solution.py:149
  5.6 1.0 shard_map.46
  6.6 40.1 %all-gather.5 = s16[4352,128]{1,0:T(8,128)(2,1)S(1)} all-gather(s16[136,128]{1,0:T(8,128)(2,1)S(1)} %shard_map.46), channel_id=2, replica_groups=mesh['x'=4,'yl'=2,'yh'=2,'z'=16,'c'=2] {'z','c'}, dimensions={0}, use_global_device_ids=true | all-gather | bytes 1148928 | tf_op jit(solution)/shard_map/all_gather | solution.py:167
  46.7 0.0 collective-permute-done.other_ref
  46.7 4.4 %shard_map.47 = s16[264,128]{1,0:T(8,128)(2,1)S(1)} custom-call(s16[16,2,136,128]{3,2,1,0:T(8,128)(2,1)S(1)} %bitcast.8, f32[64,4096]{1,0:T(8,128)} %bitcast.11, f32[64,4096]{1,0:T(8,128)S(1)} %collective-permute-done.other_ref), custom_call_target="tpu_custom_call" | custom-call | tf_op jit(solution)/shard_map/pallas_call | solution.py:169
  51.1 0.0 copy-start
  51.1 5.8 %all-gather.1 = s16[528,128]{1,0:T(8,128)(2,1)S(1)} all-gather(s16[264,128]{1,0:T(8,128)(2,1)S(1)} %shard_map.47), channel_id=3, replica_groups=mesh['x'=4,'yl'=2,'yh'=2,'z'=16,'c'=2] {'yh'}, dimensions={0}, use_global_device_ids=true | all-gather | bytes 202752 | tf_op jit(solution)/shard_map/all_gather | solution.py:182
  56.9 44.0 %all-gather.6 = s16[64,264,128]{2,1,0:T(8,128)(2,1)S(1)} all-gather(s16[2,264,128]{2,1,0:T(8,128)(2,1)S(1)} %bitcast.12), channel_id=4, replica_groups=mesh['x'=4,'yl'=2,'yh'=2,'z'=16,'c'=2] {'z','c'}, dimensions={0}, use_global_device_ids=true | all-gather | bytes 4460544 | tf_op jit(solution)/shard_map/all_gather | solution.py:183
  100.9 0.0 copy-done
  100.9 3.0 %shard_map.48 = bf16[8,64,384]{2,1,0:T(8,128)(2,1)S(1)} custom-call(s16[16,2,2,264,128]{4,3,2,1,0:T(8,128)(2,1)S(1)} %bitcast.7, bf16[384,4096]{1,0:T(8,128)(2,1)S(1)} %bitcast.9), custom_call_target="tpu_custom_call" | custom-call | tf_op jit(solution)/shard_map/pallas_call | solution.py:185
  103.9 11.8 %all_to_all.5 = bf16[8,64,384]{2,1,0:T(8,128)(2,1)S(1)} all-to-all(bf16[8,64,384]{2,1,0:T(8,128)(2,1)S(1)} %shard_map.48), channel_id=1, replica_groups=mesh['x'=4,'yl'=2,'yh'=2,'z'=16,'c'=2] {'x','yl'}, dimensions={0} | all-to-all | bytes 786432 | tf_op jit(solution)/shard_map/all_to_all | solution.py:193
  115.7 0.7 convert_reduce_fusion
Async XLA Ops:
  0.0 46.7 %collective-permute-start = (f32[64,4096]{1,0:T(8,128)}, f32[64,4096]{1,0:T(8,128)S(1)}, u32[]{:S(2)}, u32[]{:S(2)}) collective-permute-start(f32[64,4096]{1,0:T(8,128)} %bitcast.10), channel_id=1, source_target_pairs={{0,32},{32,0},{1,33},{33,1},{2,34},{34,2},{3,35},{35,3},{4,36},{36... | collective-permute-start | bytes 3145736 | tf_op jit(solution)/shard_map/ppermute | solution.py:149
  51.1 49.8 %copy-start = (bf16[1,384,4096]{2,1,0:T(8,128)(2,1)S(1)}, bf16[1,384,4096]{2,1,0:T(8,128)(2,1)}, u32[]{:S(2)}) copy-start(bf16[1,384,4096]{2,1,0:T(8,128)(2,1)} %param.7) | copy-start | bytes 9437188

commit v9 on v8

--- a/solution.py
+++ b/solution.py
@@ -11,7 +11,7 @@
 F32, BF16, I32, I16 = jnp.float32, jnp.bfloat16, jnp.int32, jnp.int16
 NT = (((1,), (1,)), ((), ()))
 VMEM = pltpu.VMEM
-UNROLL = 8
+UNROLL = 16
 ENCODE_MIB = 8
 
 
@@ -132,7 +132,7 @@
             for half, tile in ((0, low), (1, high)):
                 at = (half * nz + z) * lanes
                 p_all[yh * rows : (yh + 1) * rows, at : at + lanes] = tile.astype(BF16)
-    s = lax.dot_general(p_all[...], t_ref[...], NT, preferred_element_type=F32).astype(BF16)
+    s = lax.dot_general(t_ref[...], p_all[...], NT, preferred_element_type=F32).T.astype(BF16)
     for m in range(8):
         out_ref[m] = s[m * 64 : (m + 1) * 64, :]
 

time: 117 us -> 116 us (level)
  no operation moved by 1% of the time
where the time goes in v9:
time: 116 us
  blocking collectives  102 us (88%)
  Pallas kernels  8.02 us (7%)
  starting transfers between devices  5.63 us (5%)
    all_gather x1, blocking collectives, body(): lax.all_gather(conditioned, ('z', 'c')).reshape(16, 2, 2, 264, 128)  44 us
    all_gather x1, blocking collectives, body(): tokens = lax.all_gather(tokens, ('z', 'c')).reshape(16, 2, 136, 128)  40.1 us
    all_to_all x1, blocking collectives, body(): partial = lax.all_to_all(partial, ('x', 'yl'), 0, 0, tiled=True)  11.8 us
    all_gather x1, blocking collectives, body(): conditioned = lax.all_gather(conditioned, 'yh')  5.83 us
    ppermute x1, starting transfers between devices, swap(): return lax.ppermute(x, axis, [(0, 1), (1, 0)])  5.63 us
    pallas_call x1, Pallas kernels, body(): pl.pallas_call(condition_kernel, out_shape=jax.ShapeDtypeStruct((264, 128...  4.01 us
    pallas_call x1, Pallas kernels, body(): pl.pallas_call(score_kernel, out_shape=jax.ShapeDtypeStruct((8, 64, examp...  3.03 us
  transfers between devices with their start and end apart: 1, of which 0 were waited for; matrix products, arithmetic and copies ran while one was open for 0% of the time, Pallas kernels for 1%

profile of v9, /device:TPU:1, one launch (start us, length us, event | category | flops | bytes accessed | tf_op | source)
XLA Modules:
  0.0 116.0 jit_solution(1927232696412179674)
XLA Ops:
  0.0 5.6 %collective-permute-start = (f32[64,4096]{1,0:T(8,128)}, f32[64,4096]{1,0:T(8,128)S(1)}, u32[]{:S(2)}, u32[]{:S(2)}) collective-permute-start(f32[64,4096]{1,0:T(8,128)} %bitcast.10), channel_id=1, source_target_pairs={{0,32},{32,0},{1,33},{33,1},{2,34},{34,2},{3,35},{35,3},{4,36},{36... | collective-permute-start | bytes 3145736 | tf_op jit(solution)/shard_map/ppermute | solution.py:149
  5.6 1.0 shard_map.46
  6.6 40.1 %all-gather.5 = s16[4352,128]{1,0:T(8,128)(2,1)S(1)} all-gather(s16[136,128]{1,0:T(8,128)(2,1)S(1)} %shard_map.46), channel_id=2, replica_groups=mesh['x'=4,'yl'=2,'yh'=2,'z'=16,'c'=2] {'z','c'}, dimensions={0}, use_global_device_ids=true | all-gather | bytes 1148928 | tf_op jit(solution)/shard_map/all_gather | solution.py:167
  46.7 0.0 collective-permute-done.other_ref
  46.7 4.0 %shard_map.47 = s16[264,128]{1,0:T(8,128)(2,1)S(1)} custom-call(s16[16,2,136,128]{3,2,1,0:T(8,128)(2,1)S(1)} %bitcast.8, f32[64,4096]{1,0:T(8,128)} %bitcast.11, f32[64,4096]{1,0:T(8,128)S(1)} %collective-permute-done.other_ref), custom_call_target="tpu_custom_call" | custom-call | tf_op jit(solution)/shard_map/pallas_call | solution.py:169
  50.7 0.0 copy-start
  50.7 5.8 %all-gather.1 = s16[528,128]{1,0:T(8,128)(2,1)S(1)} all-gather(s16[264,128]{1,0:T(8,128)(2,1)S(1)} %shard_map.47), channel_id=3, replica_groups=mesh['x'=4,'yl'=2,'yh'=2,'z'=16,'c'=2] {'yh'}, dimensions={0}, use_global_device_ids=true | all-gather | bytes 202752 | tf_op jit(solution)/shard_map/all_gather | solution.py:182
  56.6 44.0 %all-gather.6 = s16[64,264,128]{2,1,0:T(8,128)(2,1)S(1)} all-gather(s16[2,264,128]{2,1,0:T(8,128)(2,1)S(1)} %bitcast.12), channel_id=4, replica_groups=mesh['x'=4,'yl'=2,'yh'=2,'z'=16,'c'=2] {'z','c'}, dimensions={0}, use_global_device_ids=true | all-gather | bytes 4460544 | tf_op jit(solution)/shard_map/all_gather | solution.py:183
  100.5 0.0 copy-done
  100.5 3.0 %shard_map.48 = bf16[8,64,384]{2,1,0:T(8,128)(2,1)S(1)} custom-call(s16[16,2,2,264,128]{4,3,2,1,0:T(8,128)(2,1)S(1)} %bitcast.7, bf16[384,4096]{1,0:T(8,128)(2,1)S(1)} %bitcast.9), custom_call_target="tpu_custom_call" | custom-call | tf_op jit(solution)/shard_map/pallas_call | solution.py:185
  103.6 11.8 %all_to_all.5 = bf16[8,64,384]{2,1,0:T(8,128)(2,1)S(1)} all-to-all(bf16[8,64,384]{2,1,0:T(8,128)(2,1)S(1)} %shard_map.48), channel_id=1, replica_groups=mesh['x'=4,'yl'=2,'yh'=2,'z'=16,'c'=2] {'x','yl'}, dimensions={0} | all-to-all | bytes 786432 | tf_op jit(solution)/shard_map/all_to_all | solution.py:193
  115.3 0.7 convert_reduce_fusion
Async XLA Ops:
  0.0 46.7 %collective-permute-start = (f32[64,4096]{1,0:T(8,128)}, f32[64,4096]{1,0:T(8,128)S(1)}, u32[]{:S(2)}, u32[]{:S(2)}) collective-permute-start(f32[64,4096]{1,0:T(8,128)} %bitcast.10), channel_id=1, source_target_pairs={{0,32},{32,0},{1,33},{33,1},{2,34},{34,2},{3,35},{35,3},{4,36},{36... | collective-permute-start | bytes 3145736 | tf_op jit(solution)/shard_map/ppermute | solution.py:149
  50.7 49.8 %copy-start = (bf16[1,384,4096]{2,1,0:T(8,128)(2,1)S(1)}, bf16[1,384,4096]{2,1,0:T(8,128)(2,1)}, u32[]{:S(2)}) copy-start(bf16[1,384,4096]{2,1,0:T(8,128)(2,1)} %param.7) | copy-start | bytes 9437188
